TPU v7x, 256 devices: a whole 4x4x8 slice. The times are simulated.
256 devices in a mesh: grp: 16 (over x, y_lo, core), inner: 16 (over y_hi, z).
Axes of the slice: x: 4, y: 4 (y_hi: 2, y_lo: 2; y = y_hi * 2 + y_lo), z: 8, core: 2. Of those that a mesh axis runs over, the one named last changes fastest.
Arguments:
- amplitudes: bfloat16 [32, 8, 12288], P('grp', None, 'inner'), may hold values from -6 to 6
- factors: bfloat16 [32, 2000, 12288], P('grp', 'inner'), may hold values from -0.125 to 0.125
- atom_charges: bfloat16 [32, 64, 12288], P('grp', None, 'inner'), may hold values from -0.0068359375 to 0.0068359375
- eps_occ: float32 [32, 48], P('grp'), may hold values from -1.2 to -0.3
- eps_vir: float32 [32, 256], P('grp'), may hold values from 0.1 to 1.5
- occ_count: int32 [32], P('grp'), may hold values from 24 to 48
- vir_count: int32 [32], P('grp'), may hold values from 128 to 256
- atom_list: int32 [2048], P('grp'), may hold values from 0 to 2047, each once
- positions: float32 [3, 2048], replicated, may hold values from 0 to 12
Outputs:
- refined: float32 [32, 8, 12288], P('grp', None, 'inner')
- hamiltonian: float32 [256, 16, 16], P('grp', None, 'inner')
Inputs may be any that keep to these rules, and one draw needn't show every extreme that they name: `atom_list`: every atom index appears exactly once.
All inputs are finite; a program needn't handle non-finite values.
Results may differ from a plain program's by a relative error of at most 0.022.
Values may be sent and summed in bfloat16 or wider, within the bound.
A program may use at most 64 MiB of HBM per device.

v0:
```python
import jax
import jax.numpy as jnp
from jax import lax
from jax.sharding import PartitionSpec as P

NVIR = 256
STATES = 8


epsilon = 1e-06


def from_everyone(shard, axis):
    peers = lax.axis_size(axis)
    return lax.all_to_all(
        jnp.broadcast_to(shard[None], (peers, *shard.shape)), axis, 0, 0, tiled=True
    )


def joined_along(pieces, dim):
    lengths = list(pieces.shape[1:])
    lengths[dim] *= pieces.shape[0]
    return jnp.moveaxis(pieces, 0, dim).reshape(lengths)


def gather_directly(shard, axis, dim):
    pieces = from_everyone(shard, axis)
    return joined_along(pieces, dim)


def cut_along(shard, dim, peers):
    lengths = shard.shape
    pieces = shard.reshape(*lengths[:dim], peers, lengths[dim] // peers, *lengths[dim + 1 :])
    return jnp.moveaxis(pieces, dim, 0)


def sum_at_owner(shard, axis, dim):
    peers = lax.axis_size(axis)
    pieces = lax.all_to_all(cut_along(shard, dim, peers), axis, 0, 0, tiled=True)
    return jnp.sum(pieces.astype(jnp.float32), axis=0)


def of_everyone(shard, axis):
    return from_everyone(shard, axis).sum(axis=0)


def together(arrays, axis):
    ravelled, at, done = (jnp.concatenate([a.reshape(-1) for a in arrays]), 0, [])
    running = of_everyone(ravelled, axis)
    for a in arrays:
        done.append(running[at : at + a.size].reshape(a.shape))
        at += a.size
    return tuple(done)


def sent_together(arrays, axis, dim, along):
    columns = [a.reshape(*a.shape[:along], -1) for a in arrays]
    both = jnp.concatenate(columns, axis=along)
    result, at, done = (lax.all_gather(both, axis, axis=dim, tiled=True), 0, [])
    for a, column in zip(arrays, columns):
        slab = result[..., at : at + column.shape[along]]
        done.append(slab.reshape(*slab.shape[:along], *a.shape[along:]))
        at += column.shape[along]
    return tuple(done)


def coupling_block(
    group_charges, own_xyz, own_ids, energies, in_charges, in_xyz, slice_rows, inner_pos, monomers
):
    count = in_charges.shape[0]
    offset = own_xyz[:, :, :, None, None] - jnp.transpose(in_xyz, (1, 0, 2))[None, :, None, :, :]
    kernel = 1.0 / jnp.sqrt(jnp.sum(offset * offset, axis=1) + 1.0)
    block = jnp.einsum("csa,carb,rb->csr", group_charges, kernel, in_charges)
    column = jnp.arange(count, dtype=jnp.int32)
    source = column // slice_rows
    within = inner_pos * slice_rows + column % slice_rows
    in_ids = source * monomers + within // STATES
    in_state = within % STATES
    same = own_ids[:, None, None] == in_ids[None, None, :]
    diag = jnp.arange(STATES, dtype=jnp.int32)[None, :, None] == in_state[None, None, :]
    block = jnp.where(same, jnp.where(diag, energies[:, :, None], 0.0), block)
    return block.reshape(monomers * STATES, count)


def local(
    amplitudes, factors, atom_charges, eps_occ, eps_vir, occ_count, vir_count, atom_list, positions
):
    monomers, states_here, local_pairs = amplitudes.shape
    atom_count = atom_charges.shape[1]
    inner_count = lax.axis_size("inner")
    inner_pos = lax.axis_index("inner")
    pair_index = inner_pos * local_pairs + jnp.arange(local_pairs, dtype=jnp.int32)
    occ_of = pair_index // NVIR
    vir_of = pair_index % NVIR
    active = (
        (occ_of[None, :] < occ_count[:, None]) & (vir_of[None, :] < vir_count[:, None])
    ).astype(jnp.float32)
    gap = jnp.take(eps_vir, vir_of, axis=1) - jnp.take(eps_occ, occ_of, axis=1)
    masked = amplitudes * active[:, None, :].astype(jnp.bfloat16)
    fitted = jnp.einsum(
        "cso,cqo->csq",
        gather_directly(masked, "inner", 2),
        factors,
        preferred_element_type=jnp.float32,
    )
    fitted_low = fitted.astype(jnp.bfloat16)
    current = masked.astype(jnp.float32)
    partial_value = (
        2.0 * jnp.einsum("csq,cqo->cso", fitted_low, factors, preferred_element_type=jnp.float32)
    ).astype(jnp.bfloat16)
    coulomb = sum_at_owner(partial_value, "inner", 2)
    image = gap[:, None, :] * current + coulomb * active[:, None, :]
    numerator, squares = together(
        (jnp.sum(current * image, axis=2), jnp.sum(current * current, axis=2)), "inner"
    )
    energies = numerator / (squares + epsilon)
    refined = active[:, None, :] * (
        current - (image - energies[:, :, None] * current) / gap[:, None, :]
    )
    refined_low = refined.astype(jnp.bfloat16)
    partial_charges = jnp.einsum(
        "cso,cao->csa", refined_low, atom_charges, preferred_element_type=jnp.float32
    ).reshape(monomers * states_here, atom_count)
    slice_rows = monomers * states_here // inner_count
    group_charges = of_everyone(partial_charges, "inner")
    slice_charges = lax.dynamic_slice_in_dim(group_charges, inner_pos * slice_rows, slice_rows, 0)
    group_charges = group_charges.reshape(monomers, states_here, atom_count)
    own_xyz = (
        jnp.take(positions, atom_list, axis=1).reshape(3, monomers, atom_count).transpose(1, 0, 2)
    )
    slice_index = inner_pos * slice_rows + jnp.arange(slice_rows, dtype=jnp.int32)
    slice_xyz = jnp.take(own_xyz, slice_index // STATES, axis=0)
    group_pos = lax.axis_index("grp")
    groups = lax.axis_size("grp")
    own_ids = group_pos * monomers + jnp.arange(monomers, dtype=jnp.int32)
    pieces = sent_together((slice_charges, slice_xyz), "grp", 0, 1)
    block = coupling_block(
        group_charges,
        own_xyz,
        own_ids,
        energies,
        pieces[0],
        pieces[1],
        slice_rows,
        inner_pos,
        monomers,
    )
    return (refined, block.reshape(monomers * states_here, groups, slice_rows))


def solution(mesh):
    in_specs = (
        P("grp", None, "inner"),
        P("grp", "inner", None),
        P("grp", None, "inner"),
        P("grp", None),
        P("grp", None),
        P("grp"),
        P("grp"),
        P("grp"),
        P(),
    )
    out_specs = (P("grp", None, "inner"), P("grp", None, "inner"))
    return jax.shard_map(local, mesh=mesh, in_specs=in_specs, out_specs=out_specs, check_vma=False)
```

profile of v0, /device:TPU:1, one launch (start us, length us, event | category | flops | bytes accessed | tf_op | source)
XLA Modules:
  0.0 116.2 jit_solution(16580661262337679980)
XLA Ops:
  0.6 0.0 copy-start
  0.7 0.8 fusion.29
  1.5 0.7 broadcast_multiply_fusion
  2.2 0.8 broadcast_in_dim.111
  3.0 11.7 %all-to-all-start = ((bf16[16,2,8,768]{3,2,1,0:T(8,128)(2,1)}), bf16[16,2,8,768]{3,2,1,0:T(8,128)(2,1)S(1)}, u32[]{:S(2)}, u32[]{:S(2)}) async-start(bf16[16,2,8,768]{3,2,1,0:T(8,128)(2,1)} %broadcast_in_dim.111), calls=%async_computation | async-start | bytes 786432 | tf_op jit(solution)/shard_map/all_to_all | solution.py:15
  14.8 0.7 compare_and_fusion.2
  15.5 0.1 broadcast_in_dim.119
  15.6 0.8 copy.49
  16.3 0.8 copy.48
  17.1 1.6 %gather_fusion = f32[768,2]{1,0:T(8,128)S(1)} fusion(f32[2,256]{0,1:T(8,128)S(1)} %copy.48, s32[1024]{0:T(1024)S(1)} %pad_clamp_fusion.2), kind=kCustom, calls=%fused_computation | custom fusion | bytes 15360 | tf_op jit(solution)/shard_map/jit(_take)/gather | solution.py:98
  18.7 1.6 %gather_fusion.1 = f32[768,2]{1,0:T(8,128)S(1)} fusion(f32[2,48]{0,1:T(8,128)S(1)} %copy.49, s32[1024]{0:T(1024)S(1)} %pad_clamp_fusion.1), kind=kCustom, calls=%fused_computation.1 | custom fusion | bytes 15360 | tf_op jit(solution)/shard_map/jit(_take)/gather | solution.py:98
  20.3 0.3 subtract_bitcast_fusion
  20.6 0.1 copy.50
  20.8 1.1 copy.56
  21.9 0.7 compare_select_fusion.7
  22.6 4.4 %all-to-all-done = bf16[16,2,8,768]{3,2,1,0:T(8,128)(2,1)S(1)} async-done(((bf16[16,2,8,768]{3,2,1,0:T(8,128)(2,1)}), bf16[16,2,8,768]{3,2,1,0:T(8,128)(2,1)S(1)}, u32[]{:S(2)}, u32[]{:S(2)}) %all-to-all-start) | async-done | bytes 393248 | tf_op jit(solution)/shard_map/all_to_all | solution.py:15
  27.0 0.0 copy-start.1
  27.0 14.3 %fusion = bf16[2,8,12288]{2,1,0:T(8,128)(2,1)S(1)} fusion(bf16[2,125,12288]{2,0,1:T(2,128)(2,1)} %param.10, bf16[2,8,12288]{2,1,0:T(8,128)(2,1)S(1)} %bitcast.52), kind=kOutput, calls=%fused_computation.4 | convolution fusion | flops 98699216 | bytes 6930432 | tf_op jit(solution)/shard_map/csq,cqo->cso/dot_general | solution.py:109
  41.3 0.8 copy.81
  42.1 6.4 %all-to-all-start.1 = ((bf16[16,2,8,768]{3,2,1,0:T(8,128)(2,1)}), bf16[16,2,8,768]{3,2,1,0:T(8,128)(2,1)S(1)}, u32[]{:S(2)}, u32[]{:S(2)}) async-start(bf16[16,2,8,768]{3,2,1,0:T(8,128)(2,1)} %bitcast.50), calls=%async_computation.1 | async-start | bytes 786432 | tf_op jit(solution)/shard_map/all_to_all | solution.py:39
  48.5 0.6 gather_fusion.2
  49.1 0.1 copy.57
  49.3 11.5 %all-to-all-done.1 = bf16[16,2,8,768]{3,2,1,0:T(8,128)(2,1)S(1)} async-done(((bf16[16,2,8,768]{3,2,1,0:T(8,128)(2,1)}), bf16[16,2,8,768]{3,2,1,0:T(8,128)(2,1)S(1)}, u32[]{:S(2)}, u32[]{:S(2)}) %all-to-all-start.1) | async-done | bytes 393248 | tf_op jit(solution)/shard_map/all_to_all | solution.py:39
  60.8 0.1 convert_reduce_fusion
  60.9 0.0 copy-done.1
  60.9 0.1 fusion.12
  61.0 0.1 reshape.402
  61.1 0.1 reshape.403
  61.1 0.1 pad_maximum_fusion
  61.2 0.6 broadcast_in_dim.112
  61.8 5.9 %all-to-all-start.2 = ((f32[16,1,32]{2,1,0:T(1,128)}), f32[16,1,32]{2,1,0:T(1,128)S(1)}, u32[]{:S(2)}, u32[]{:S(2)}) async-start(f32[16,1,32]{2,1,0:T(1,128)} %broadcast_in_dim.112), calls=%async_computation.2 | async-start | bytes 16384 | tf_op jit(solution)/shard_map/all_to_all | solution.py:15
  67.7 0.1 broadcast_compare_fusion
  67.8 8.7 %all-to-all-done.2 = f32[16,1,32]{2,1,0:T(1,128)S(1)} async-done(((f32[16,1,32]{2,1,0:T(1,128)}), f32[16,1,32]{2,1,0:T(1,128)S(1)}, u32[]{:S(2)}, u32[]{:S(2)}) %all-to-all-start.2) | async-done | bytes 2080 | tf_op jit(solution)/shard_map/all_to_all | solution.py:15
  76.5 0.1 add_divide_fusion
  76.6 0.1 div.68
  76.6 0.1 fusion.16
  76.7 0.0 copy-done
  76.7 0.0 copy-start.2
  76.8 0.1 convolution_bitcast_fusion
  76.9 0.7 reshape.470
  77.7 3.5 %all-to-all-start.3 = ((f32[16,1,1024]{2,1,0:T(1,128)}), f32[16,1,1024]{2,1,0:T(1,128)S(1)}, u32[]{:S(2)}, u32[]{:S(2)}) async-start(f32[16,1,1024]{2,1,0:T(1,128)} %reshape.470), calls=%async_computation.3 | async-start | bytes 131072 | tf_op jit(solution)/shard_map/all_to_all | solution.py:15
  81.2 0.1 select_n.179
  81.3 8.7 %all-to-all-done.3 = f32[16,1,1024]{2,1,0:T(1,128)S(1)} async-done(((f32[16,1,1024]{2,1,0:T(1,128)}), f32[16,1,1024]{2,1,0:T(1,128)S(1)}, u32[]{:S(2)}, u32[]{:S(2)}) %all-to-all-start.3) | async-done | bytes 65568 | tf_op jit(solution)/shard_map/all_to_all | solution.py:15
  90.0 0.5 broadcast.647
  90.5 0.8 reduce.5
  91.3 0.1 reshape.471
  91.5 0.1 maximum_bitcast_fusion
  91.5 22.6 %all-gather = f32[16,1,256]{2,1,0:T(1,128)S(1)} all-gather(f32[1,1,256]{2,1,0:T(1,128)S(1)} %maximum_bitcast_fusion), channel_id=1, replica_groups=mesh['grp'=16,'inner'=16] {'grp'}, dimensions={0}, use_global_device_ids=true | all-gather | bytes 17408 | tf_op jit(solution)/shard_map/all_gather | solution.py:59
  114.2 0.1 slice.47
  114.3 0.1 reshape.405
  114.4 0.5 multiply_reduce_fusion
  114.8 0.1 add_rsqrt_fusion
  115.0 0.5 fusion.9
  115.5 0.8 convolution_select_fusion
  116.2 0.0 copy-done.2
  (20 shorter events, 0.2 us)
Async XLA Ops:
  0.6 76.1 %copy-start = (bf16[2,64,768]{2,1,0:T(8,128)(2,1)S(1)}, bf16[2,64,768]{2,1,0:T(8,128)(2,1)}, u32[]{:S(2)}) copy-start(bf16[2,64,768]{2,1,0:T(8,128)(2,1)} %param.11) | copy-start | bytes 589828
  3.0 24.0 %all-to-all-start = ((bf16[16,2,8,768]{3,2,1,0:T(8,128)(2,1)}), bf16[16,2,8,768]{3,2,1,0:T(8,128)(2,1)S(1)}, u32[]{:S(2)}, u32[]{:S(2)}) async-start(bf16[16,2,8,768]{3,2,1,0:T(8,128)(2,1)} %broadcast_in_dim.111), calls=%async_computation | async-start | bytes 786432 | tf_op jit(solution)/shard_map/all_to_all | solution.py:15
  27.0 33.9 %copy-start.1 = (bf16[2,8,768]{2,1,0:T(8,128)(2,1)S(1)}, bf16[2,8,768]{2,1,0:T(8,128)(2,1)}, u32[]{:S(2)}) copy-start(bf16[2,8,768]{2,1,0:T(8,128)(2,1)} %param.9) | copy-start | bytes 73732
  42.1 18.7 %all-to-all-start.1 = ((bf16[16,2,8,768]{3,2,1,0:T(8,128)(2,1)}), bf16[16,2,8,768]{3,2,1,0:T(8,128)(2,1)S(1)}, u32[]{:S(2)}, u32[]{:S(2)}) async-start(bf16[16,2,8,768]{3,2,1,0:T(8,128)(2,1)} %bitcast.50), calls=%async_computation.1 | async-start | bytes 786432 | tf_op jit(solution)/shard_map/all_to_all | solution.py:39
  61.8 14.6 %all-to-all-start.2 = ((f32[16,1,32]{2,1,0:T(1,128)}), f32[16,1,32]{2,1,0:T(1,128)S(1)}, u32[]{:S(2)}, u32[]{:S(2)}) async-start(f32[16,1,32]{2,1,0:T(1,128)} %broadcast_in_dim.112), calls=%async_computation.2 | async-start | bytes 16384 | tf_op jit(solution)/shard_map/all_to_all | solution.py:15
  76.7 39.5 %copy-start.2 = (f32[2,8,768]{2,1,0:T(8,128)}, f32[2,8,768]{2,1,0:T(8,128)S(1)}, u32[]{:S(2)}) copy-start(f32[2,8,768]{2,1,0:T(8,128)S(1)} %fusion.16) | copy-start | bytes 147460
  77.7 12.3 %all-to-all-start.3 = ((f32[16,1,1024]{2,1,0:T(1,128)}), f32[16,1,1024]{2,1,0:T(1,128)S(1)}, u32[]{:S(2)}, u32[]{:S(2)}) async-start(f32[16,1,1024]{2,1,0:T(1,128)} %reshape.470), calls=%async_computation.3 | async-start | bytes 131072 | tf_op jit(solution)/shard_map/all_to_all | solution.py:15
where the time goes:
time: 117 us; the launch traced here: 116 us
  waiting for transfers between devices  33.4 us (29%)
  starting transfers between devices  27.5 us (24%)
  blocking collectives  22.6 us (19%)
  matrix products  15.7 us (13%)
  local copies, waits for them, and re-layouts  10.9 us (9%)
  other arithmetic  5.29 us (5%)
    all_gather x1, blocking collectives, sent_together(): result, at, done = (lax.all_gather(both, axis, axis=dim, tiled=True), 0, [])  22.6 us
    all_to_all x3, waiting for transfers between devices, from_everyone(): lax.all_to_all(jnp.broadcast_to(shard[None], (peers, *shard.shape)), axis...  21.8 us
    all_to_all x3, starting transfers between devices, from_everyone(): lax.all_to_all(jnp.broadcast_to(shard[None], (peers, *shard.shape)), axis...  21.1 us
    dot_general x1, matrix products, local(): jnp.einsum('csq,cqo->cso', fitted_low, factors, preferred_element_type=jn...  14.3 us
    all_to_all x1, waiting for transfers between devices, sum_at_owner(): lax.all_to_all(cut_along(shard, dim, peers), axis, 0, 0, tiled=True)  11.5 us
    all_to_all x1, starting transfers between devices, sum_at_owner(): lax.all_to_all(cut_along(shard, dim, peers), axis, 0, 0, tiled=True)  6.39 us
    unnamed x12, local copies, waits for them, and re-layouts  3.56 us
    gather x2, local copies, waits for them, and re-layouts, local(): gap = jnp.take(eps_vir, vir_of, axis=1) - jnp.take(eps_occ, occ_of, axis=1)  3.15 us
  transfers between devices with their start and end apart: 4, of which 4 were waited for; matrix products, arithmetic and copies ran while one was open for 7% of the time, Pallas kernels for 0%

commit v1 on v0

v1 whole, which is shorter than its diff:
```python
import functools

import jax
import jax.numpy as jnp
from jax import lax
from jax.experimental import pallas as pl
from jax.experimental.pallas import tpu as pltpu
from jax.sharding import PartitionSpec as P

NVIR = 256
STATES = 8
EPSILON = 1e-06
Z = 8
MESH = pl.DeviceIdType.MESH
PEERS = sorted(
    [(dy, dz) for dy in (0, 1) for dz in range(Z) if (dy, dz) != (0, 0)],
    key=lambda r: -(2 * r[0] + min(r[1], Z - r[1])),
)
N_IN = len(PEERS)
N_GRP = 15
NT = (((1,), (1,)), ((), ()))
NN = (((1,), (0,)), ((), ()))


def split(x):
    high = x.astype(jnp.bfloat16)
    return high, (x - high.astype(jnp.float32)).astype(jnp.bfloat16)


def dot(a, b, dims):
    return lax.dot_general(a, b, dims, preferred_element_type=jnp.float32)


def inner_at(rel, sign):
    me = lax.axis_index("inner")
    y, z = me // Z, me % Z
    return lax.rem(y + rel[0], 2) * Z + lax.rem(z + sign * rel[1] + Z, Z)


def grp_at(step, sign):
    return lax.rem(lax.axis_index("grp") + sign * step + 16, 16)


def remote(src, dst, sems, n, axis, where):
    return pltpu.make_async_remote_copy(
        src_ref=src,
        dst_ref=dst,
        send_sem=sems.at[0, n],
        recv_sem=sems.at[1, n],
        device_id={axis: where},
        device_id_type=MESH,
    )


def kernel(
    amp_ref, fac_hbm, chg_ref, occ_e, vir_e, occ_n, vir_n, atoms_ref, pos_ref,
    refined_ref, block_ref,
    fac, amp_land, part, part_land, e_send, e_land, c_send, c_land, g_send, g_land, x_send, x_land,
    pos8, k_hi, k_lo, fac_sem, amp_sem, part_sem, e_sem, c_sem, g_sem, x_sem,
):
    me = lax.axis_index("inner")
    grp = lax.axis_index("grp")
    rows_n, pairs = amp_ref.shape
    segs = pairs // NVIR
    aux, tiles = fac_hbm.shape[:2]

    barrier = pltpu.get_barrier_semaphore()
    for rel in PEERS:
        pl.semaphore_signal(barrier, inc=1, device_id={"inner": inner_at(rel, 1)}, device_id_type=MESH)
    for a in range(1, 16):
        pl.semaphore_signal(barrier, inc=1, device_id={"grp": grp_at(a, 1)}, device_id_type=MESH)
    loads = []
    for j in range(tiles):
        fac[j, aux:128] = jnp.zeros((128 - aux, 2, 128), jnp.bfloat16)
        loads.append(pltpu.make_async_copy(fac_hbm.at[:, j], fac.at[j, pl.ds(0, aux)], fac_sem))
        loads[-1].start()
    flat = fac.reshape(tiles, 256, 128)
    per = pairs // 128

    def piece(who):
        return jnp.concatenate([flat[who * per + m] for m in range(per)], axis=1)

    pos8[...] = jnp.zeros_like(pos8)
    pos8[0:3, :] = pos_ref[...]
    p_all = pos8[...]
    p_hi = p_all.astype(jnp.bfloat16)
    rest = p_all - p_hi.astype(jnp.float32)
    p_mid = rest.astype(jnp.bfloat16)
    p_lo = (rest - p_mid.astype(jnp.float32)).astype(jnp.bfloat16)
    table = pos_ref.shape[1]
    hot = (
        (lax.broadcasted_iota(jnp.int32, (table, 128), 0) == atoms_ref[...])
        .astype(jnp.float32)
        .astype(jnp.bfloat16)
    )
    own_xyz = dot(p_hi, hot, NN) + dot(p_mid, hot, NN) + dot(p_lo, hot, NN)
    x_send[...] = own_xyz

    pl.semaphore_wait(barrier, N_IN + N_GRP)

    amp_copies = [
        remote(amp_ref, amp_land.at[n], amp_sem, n, "inner", inner_at(rel, 1))
        for n, rel in enumerate(PEERS)
    ]
    for c in amp_copies:
        c.start()
    x_copies = [
        remote(x_send, x_land.at[a - 1], x_sem, a - 1, "grp", grp_at(a, 1)) for a in range(1, 16)
    ]
    for c in x_copies:
        c.start()

    lane = lax.broadcasted_iota(jnp.int32, (STATES, pairs), 1)
    seg, vir = lane // NVIR, lane % NVIR
    vir_in = [vir < vir_n[c] for c in range(2)]

    def active_of(who):
        return jnp.concatenate(
            [jnp.where(vir_in[c] & (seg + who * segs < occ_n[c]), 1.0, 0.0) for c in range(2)],
            axis=0,
        )

    active = active_of(me)
    gap = jnp.concatenate(
        [
            jnp.concatenate(
                [
                    jnp.broadcast_to(vir_e[c : c + 1, :] - occ_e[c, me * segs + m], (STATES, NVIR))
                    for m in range(segs)
                ],
                axis=1,
            )
            for c in range(2)
        ],
        axis=0,
    )
    masked = amp_ref[...].astype(jnp.float32) * active

    for c in loads:
        c.wait()

    fitted = dot(masked.astype(jnp.bfloat16), piece(me), NT)
    for n in reversed(range(N_IN)):
        amp_copies[n].wait_recv()
        who = inner_at(PEERS[n], -1)
        theirs = (amp_land[n].astype(jnp.float32) * active_of(who)).astype(jnp.bfloat16)
        fitted = fitted + dot(theirs, piece(who), NT)
    parity = lax.broadcasted_iota(jnp.int32, fitted.shape, 1) % 2
    monomer = lax.broadcasted_iota(jnp.int32, fitted.shape, 0) // STATES
    fitted = jnp.where(parity == monomer, fitted, 0.0)
    low = fitted.astype(jnp.bfloat16)

    row16 = lax.broadcasted_iota(jnp.int32, (rows_n, 128), 0)
    lane16 = lax.broadcasted_iota(jnp.int32, (rows_n, 128), 1)
    num = jnp.sum(gap * masked * masked, axis=1, keepdims=True) + 2.0 * jnp.sum(
        low.astype(jnp.float32) * fitted, axis=1, keepdims=True
    )
    sq = jnp.sum(masked * masked, axis=1, keepdims=True)
    tile = jnp.where(lane16 == row16, num, 0.0) + jnp.where(lane16 == row16 + 16, sq, 0.0)
    e_row = jnp.sum(tile, axis=0, keepdims=True)
    e_send[...] = e_row
    e_copies = [
        remote(e_send, e_land.at[n], e_sem, n, "inner", inner_at(rel, 1))
        for n, rel in enumerate(PEERS)
    ]
    for c in e_copies:
        c.start()

    part_copies = []
    for n, rel in enumerate(PEERS):
        who = inner_at(rel, 1)
        part[n] = (2.0 * dot(low, piece(who), NN)).astype(jnp.bfloat16)
        copy = remote(part.at[n], part_land.at[n], part_sem, n, "inner", who)
        copy.start()
        part_copies.append(copy)
    coulomb = (2.0 * dot(low, piece(me), NN)).astype(jnp.bfloat16).astype(jnp.float32)

    own_cols = jnp.transpose(own_xyz)
    for a in range(16):
        if a > 0:
            x_copies[a - 1].wait_recv()
        there = own_xyz if a == 0 else x_land[a - 1]
        r2 = jnp.zeros((128, 128), jnp.float32)
        for k in range(3):
            d = own_cols[:, k : k + 1] - there[k : k + 1, :]
            r2 = r2 + d * d
        hi, lo = split(lax.rsqrt(r2 + 1.0))
        k_hi[:, a * 128 : (a + 1) * 128] = hi
        k_lo[:, a * 128 : (a + 1) * 128] = lo

    for copy in e_copies:
        copy.wait_recv()
    total = e_row
    for n in range(N_IN):
        total = total + e_land[n]
    num = jnp.sum(jnp.where(lane16 == row16, total, 0.0), axis=1, keepdims=True)
    sq = jnp.sum(jnp.where(lane16 == row16 + 16, total, 0.0), axis=1, keepdims=True)
    energy = num / (sq + EPSILON)

    for n in reversed(range(N_IN)):
        part_copies[n].wait_recv()
        coulomb = coulomb + part_land[n].astype(jnp.float32)

    sigma = gap * masked + active * coulomb
    refined = active * (masked - (sigma - energy * masked) / gap)
    refined_ref[...] = refined
    both = dot(refined.astype(jnp.bfloat16), chg_ref[...], NT)
    first = lane16[0:STATES] < 64
    own = jnp.where(first, both[0:STATES], both[STATES:])
    c_send[...] = own
    c_copies = [
        remote(c_send, c_land.at[n], c_sem, n, "inner", inner_at(rel, 1))
        for n, rel in enumerate(PEERS)
    ]
    for c in c_copies:
        c.start()
    charges = own
    for n in reversed(range(N_IN)):
        c_copies[n].wait_recv()
        charges = charges + c_land[n]
    g_send[...] = charges
    g_copies = [
        remote(g_send, g_land.at[a - 1], g_sem, a - 1, "grp", grp_at(a, 1)) for a in range(1, 16)
    ]
    for c in g_copies:
        c.start()

    rows = jnp.concatenate([jnp.where(first, charges, 0.0), jnp.where(first, 0.0, charges)], axis=0)
    rows_hi, rows_lo = split(rows)
    with_hi = dot(jnp.concatenate([rows_hi, rows_lo], axis=0), k_hi[...], NN)
    field = with_hi[0:16] + with_hi[16:32] + dot(rows_hi, k_lo[...], NN)

    t = lax.rem(me, STATES)
    half = me // STATES
    in_half = (lax.broadcasted_iota(jnp.int32, (1, 128), 1) // 64) == half
    out_lane = lax.broadcasted_iota(jnp.int32, (16, 16), 1)
    block = jnp.zeros((16, 16), jnp.float32)
    for a in range(16):
        if a > 0:
            g_copies[a - 1].wait_recv()
        src = g_send if a == 0 else g_land.at[a - 1]
        q = jnp.where(in_half, src[pl.ds(t, 1), :], 0.0)
        column = jnp.sum(field[:, a * 128 : (a + 1) * 128] * q, axis=1, keepdims=True)
        block = jnp.where(out_lane == grp_at(a, -1), column, block)
    out_row = lax.broadcasted_iota(jnp.int32, (16, 16), 0)
    same = (out_lane == grp) & (out_row // STATES == half)
    block_ref[...] = jnp.where(same, jnp.where(out_row % STATES == t, energy, 0.0), block)

    for copies in (amp_copies, x_copies, e_copies, part_copies, c_copies, g_copies):
        for c in copies:
            c.wait_send()


def local(
    amplitudes, factors, atom_charges, eps_occ, eps_vir, occ_count, vir_count, atom_list, positions
):
    monomers, states, pairs = amplitudes.shape
    aux, every = factors.shape[1:]
    rows = monomers * states
    vmem = pl.BlockSpec(memory_space=pltpu.VMEM)
    smem = pl.BlockSpec(memory_space=pltpu.SMEM)
    bf, f32 = jnp.bfloat16, jnp.float32
    by_tile = jnp.transpose(factors, (1, 0, 2)).reshape(aux, monomers, every // 128, 128)
    refined, block = pl.pallas_call(
        kernel,
        name="exciton",
        out_shape=(
            jax.ShapeDtypeStruct((rows, pairs), f32),
            jax.ShapeDtypeStruct((rows, rows), f32),
        ),
        in_specs=[vmem, pl.BlockSpec(memory_space=pl.ANY), vmem, smem, vmem, smem, smem, vmem, vmem],
        out_specs=(vmem, vmem),
        scratch_shapes=[
            pltpu.VMEM((every // 128, 128, monomers, 128), bf),
            pltpu.VMEM((N_IN, rows, pairs), bf),
            pltpu.VMEM((N_IN, rows, pairs), bf),
            pltpu.VMEM((N_IN, rows, pairs), bf),
            pltpu.VMEM((1, 128), f32),
            pltpu.VMEM((N_IN, 1, 128), f32),
            pltpu.VMEM((8, 128), f32),
            pltpu.VMEM((N_IN, 8, 128), f32),
            pltpu.VMEM((8, 128), f32),
            pltpu.VMEM((N_GRP, 8, 128), f32),
            pltpu.VMEM((8, 128), f32),
            pltpu.VMEM((N_GRP, 8, 128), f32),
            pltpu.VMEM((8, positions.shape[1]), f32),
            pltpu.VMEM((128, 2048), bf),
            pltpu.VMEM((128, 2048), bf),
            pltpu.SemaphoreType.DMA,
        ]
        + [pltpu.SemaphoreType.DMA((2, 15))] * 6,
        compiler_params=pltpu.CompilerParams(collective_id=0, has_side_effects=True),
    )(
        amplitudes.reshape(rows, pairs),
        by_tile.transpose(0, 2, 1, 3),
        atom_charges.reshape(monomers * 64, pairs),
        eps_occ, eps_vir, occ_count, vir_count, atom_list.reshape(1, -1), positions,
    )
    return refined.reshape(monomers, states, pairs), block.reshape(rows, rows, 1)


def solution(mesh):
    in_specs = (
        P("grp", None, "inner"),
        P("grp", "inner", None),
        P("grp", None, "inner"),
        P("grp", None),
        P("grp", None),
        P("grp"),
        P("grp"),
        P("grp"),
        P(),
    )
    out_specs = (P("grp", None, "inner"), P("grp", None, "inner"))
    return jax.shard_map(local, mesh=mesh, in_specs=in_specs, out_specs=out_specs, check_vma=False)
```

time: 117 us -> 54.5 us (0.47)
  Pallas kernels: 0 us -> 51 us
  waiting for transfers between devices: 33.4 us -> 0 us
  starting transfers between devices: 27.5 us -> 0 us
  blocking collectives: 22.6 us -> 0 us
  matrix products: 15.7 us -> 0 us
  local copies, waits for them, and re-layouts: 10.9 us -> 2.72 us
  other arithmetic: 5.29 us -> 0 us
    pallas_call x0 -> x1, Pallas kernels: none -> 51 us  [local(): pl.pallas_call(kernel, name='exciton', out_shape=(jax.ShapeDtypeStruct((r...]
    all_to_all x4 -> x0, waiting for transfers between devices: 33.4 us -> none  [the longest x3 21.8 us: from_everyone(): lax.all_to_all(jnp.broadcast_to(shard[None], (peers, *shard.shape)), axis...]
    all_to_all x4 -> x0, starting transfers between devices: 27.5 us -> none  [the longest x3 21.1 us: from_everyone(): lax.all_to_all(jnp.broadcast_to(shard[None], (peers, *shard.shape)), axis...]
    all_gather x1 -> x0, blocking collectives: 22.6 us -> none  [sent_together(): result, at, done = (lax.all_gather(both, axis, axis=dim, tiled=True), 0, [])]
    dot_general x4 -> x0, matrix products: 15.7 us -> none  [the longest x1 14.3 us: local(): jnp.einsum('csq,cqo->cso', fitted_low, factors, preferred_element_type=jn...]
    gather x4 -> x0, local copies, waits for them, and re-layouts: 3.87 us -> none  [the longest x2 3.15 us: local(): gap = jnp.take(eps_vir, vir_of, axis=1) - jnp.take(eps_occ, occ_of, axis=1)]
    broadcast_in_dim x4 -> x0, local copies, waits for them, and re-layouts: 1.48 us -> none  [the longest x3 1.4 us: from_everyone(): jnp.broadcast_to(shard[None], (peers, *shard.shape))]
    unnamed x12 -> x2, local copies, waits for them, and re-layouts: 3.56 us -> 2.72 us
  transfers between devices with their start and end apart: 4 -> 0, of which waited for: 4 -> 0; matrix products, arithmetic and copies ran while one was open for 7% -> 0% of each run, Pallas kernels for 0% -> 0%
where the time goes in v1:
time: 54.5 us; the launch traced here: 54.3 us
  Pallas kernels  51 us (94%)
  local copies, waits for them, and re-layouts  2.72 us (5%)
  between operations  0.64 us (1%)
    pallas_call x1, Pallas kernels, local(): pl.pallas_call(kernel, name='exciton', out_shape=(jax.ShapeDtypeStruct((r...  51 us
    unnamed x2, local copies, waits for them, and re-layouts  2.72 us

profile of v1, /device:TPU:1, one launch (start us, length us, event | category | flops | bytes accessed | tf_op | source)
XLA Modules:
  0.0 54.3 jit_solution(2294607046688703837)
XLA Ops:
  0.6 51.0 %exciton.1 = (f32[16,768]{1,0:T(8,128)}, f32[16,16]{1,0:T(8,128)}) custom-call(bf16[16,768]{1,0:T(8,128)(2,1)} %bitcast.15, bf16[125,96,2,128]{3,2,1,0:T(2,128)(2,1)} %bitcast.12, bf16[128,768]{1,0:T(8,128)(2,1)} %bitcast.13, f32[2,48]{1,0:T(2,128)} %occ_e.1, f32[2,256]{1,0:T(2,128)} %vir_e.1, s32[2]{0:T(128)} %occ_n.1, s32[2]{0:T(128)} %vir_n.1, ...), custom_call_target="tpu_custom_call" | custom-call | tf_op jit(solution)/shard_map/exciton/pallas_call | solution.py:264
  51.6 1.4 %copy.14 = f32[2,8,768]{2,1,0:T(8,128)} copy(f32[2,8,768]{2,1,0:T(8,128)} %bitcast.14) | data formatting | bytes 98304
  53.0 1.3 %copy.15 = f32[16,16,1]{1,2,0:T(1,128)} copy(f32[16,16,1]{1,2,0:T(1,128)} %bitcast.16) | data formatting | bytes 2048

commit v2 on v1

v2 whole, which is shorter than its diff:
```python
import jax
import jax.numpy as jnp
from jax import lax
from jax.experimental import pallas as pl
from jax.experimental.pallas import tpu as pltpu
from jax.sharding import PartitionSpec as P

NVIR = 256
STATES = 8
EPSILON = 1e-06
Z = 8
MESH = pl.DeviceIdType.MESH
FAR_Z = (4, 3, 5, 2, 6, 1, 7)
PEERS = sorted(
    [(dy, dz) for dy in (0, 1) for dz in range(Z) if (dy, dz) != (0, 0)],
    key=lambda r: -(2 * r[0] + min(r[1], Z - r[1])),
)
N_IN = len(PEERS)
N_Z = len(FAR_Z)
N_GRP = 15
NT = (((1,), (1,)), ((), ()))
NN = (((1,), (0,)), ((), ()))


def split(x):
    high = x.astype(jnp.bfloat16)
    return high, (x - high.astype(jnp.float32)).astype(jnp.bfloat16)


def dot(a, b, dims):
    return lax.dot_general(a, b, dims, preferred_element_type=jnp.float32)


def inner_at(rel, sign):
    me = lax.axis_index("inner")
    y, z = me // Z, me % Z
    return lax.rem(y + rel[0], 2) * Z + lax.rem(z + sign * rel[1] + Z, Z)


def grp_at(step, sign):
    return lax.rem(lax.axis_index("grp") + sign * step + 16, 16)


def remote(src, dst, sems, n, axis, where):
    return pltpu.make_async_remote_copy(
        src_ref=src,
        dst_ref=dst,
        send_sem=sems.at[0, n],
        recv_sem=sems.at[1, n],
        device_id={axis: where},
        device_id_type=MESH,
    )


def start_all(copies):
    for c in copies:
        c.start()
    return copies


def kernel(
    amp_hbm, fac_hbm, chg_hbm, occ_e_hbm, vir_e_hbm, occ_n_hbm, vir_n_hbm, atoms_hbm, pos_hbm,
    refined_ref, block_ref,
    amp_ref, chg_ref, occ_e, vir_e, occ_n, vir_n, atoms_ref, pos_ref,
    fac, amp_y, amp_z, amp_yz, part_y, land_y, part_z, land_z,
    e_send, e_land, c_send, c_land, g_send, g_land, x_send, x_land, pos8, k_hi, k_lo,
    in_sem, fac_sem, ay_sem, az_sem, ayz_sem, py_sem, pz_sem, e_sem, c_sem, g_sem, x_sem,
):
    me = lax.axis_index("inner")
    grp = lax.axis_index("grp")
    rows_n, pairs = amp_ref.shape
    segs = pairs // NVIR
    aux, tiles = fac_hbm.shape[:2]
    per = pairs // 128

    barrier = pltpu.get_barrier_semaphore()
    for rel in [(1, 0)] + [(0, dz) for dz in FAR_Z]:
        pl.semaphore_signal(barrier, inc=1, device_id={"inner": inner_at(rel, 1)}, device_id_type=MESH)
    for a in range(1, 16):
        pl.semaphore_signal(barrier, inc=1, device_id={"grp": grp_at(a, 1)}, device_id_type=MESH)
    pairs_in = [
        (amp_hbm, amp_ref), (vir_e_hbm, vir_e), (occ_e_hbm, occ_e), (occ_n_hbm, occ_n),
        (vir_n_hbm, vir_n), (atoms_hbm, atoms_ref), (pos_hbm, pos_ref), (chg_hbm, chg_ref),
    ]
    inputs = start_all(
        [pltpu.make_async_copy(src, dst, in_sem.at[n]) for n, (src, dst) in enumerate(pairs_in)]
    )
    inputs[0].wait()
    pl.semaphore_wait(barrier, 1 + N_Z + N_GRP)

    to_y = remote(amp_ref, amp_y, ay_sem, 0, "inner", inner_at((1, 0), 1))
    to_y.start()
    to_z = start_all(
        [
            remote(amp_ref, amp_z.at[n], az_sem, n, "inner", inner_at((0, dz), 1))
            for n, dz in enumerate(FAR_Z)
        ]
    )
    loads = []
    for j in range(tiles):
        loads.append(pltpu.make_async_copy(fac_hbm.at[:, j], fac.at[j, pl.ds(0, aux)], fac_sem))
        loads[-1].start()
    to_y.wait_recv()
    onward = start_all(
        [
            remote(amp_y, amp_yz.at[n], ayz_sem, n, "inner", inner_at((0, dz), 1))
            for n, dz in enumerate(FAR_Z)
        ]
    )
    for copy in inputs[1:]:
        copy.wait()
    for j in range(tiles):
        fac[j, aux:128] = jnp.zeros((128 - aux, 2, 128), jnp.bfloat16)
    flat = fac.reshape(tiles, 256, 128)

    def piece(who):
        return jnp.concatenate([flat[who * per + m] for m in range(per)], axis=1)

    pos8[...] = jnp.zeros_like(pos8)
    pos8[0:3, :] = pos_ref[...]
    p_all = pos8[...]
    p_hi = p_all.astype(jnp.bfloat16)
    rest = p_all - p_hi.astype(jnp.float32)
    p_mid = rest.astype(jnp.bfloat16)
    p_lo = (rest - p_mid.astype(jnp.float32)).astype(jnp.bfloat16)
    hot = (
        (lax.broadcasted_iota(jnp.int32, (pos_ref.shape[1], 128), 0) == atoms_ref[...])
        .astype(jnp.float32)
        .astype(jnp.bfloat16)
    )
    own_xyz = dot(p_hi, hot, NN) + dot(p_mid, hot, NN) + dot(p_lo, hot, NN)
    x_send[...] = own_xyz
    x_copies = start_all(
        [remote(x_send, x_land.at[a - 1], x_sem, a - 1, "grp", grp_at(a, 1)) for a in range(1, 16)]
    )

    lane = lax.broadcasted_iota(jnp.int32, (STATES, pairs), 1)
    seg, vir = lane // NVIR, lane % NVIR
    vir_in = [vir < vir_n[c] for c in range(2)]

    def active_of(who):
        return jnp.concatenate(
            [jnp.where(vir_in[c] & (seg + who * segs < occ_n[c]), 1.0, 0.0) for c in range(2)],
            axis=0,
        )

    active = active_of(me)
    gap = jnp.concatenate(
        [
            jnp.concatenate(
                [
                    jnp.broadcast_to(vir_e[c : c + 1, :] - occ_e[c, me * segs + m], (STATES, NVIR))
                    for m in range(segs)
                ],
                axis=1,
            )
            for c in range(2)
        ],
        axis=0,
    )
    masked = amp_ref[...].astype(jnp.float32) * active

    for c in loads:
        c.wait()

    def fit(amps, who):
        theirs = (amps.astype(jnp.float32) * active_of(who)).astype(jnp.bfloat16)
        return dot(theirs, piece(who), NT)

    fitted = dot(masked.astype(jnp.bfloat16), piece(me), NT)
    fitted = fitted + fit(amp_y[...], inner_at((1, 0), 1))
    for n in reversed(range(N_Z)):
        to_z[n].wait_recv()
        fitted = fitted + fit(amp_z[n], inner_at((0, FAR_Z[n]), -1))
    for n in reversed(range(N_Z)):
        onward[n].wait_recv()
        fitted = fitted + fit(amp_yz[n], inner_at((1, FAR_Z[n]), -1))
    parity = lax.broadcasted_iota(jnp.int32, fitted.shape, 1) % 2
    monomer = lax.broadcasted_iota(jnp.int32, fitted.shape, 0) // STATES
    fitted = jnp.where(parity == monomer, fitted, 0.0)
    low = fitted.astype(jnp.bfloat16)

    order = FAR_Z + (0,)
    cross = []
    for n, dz in enumerate(order):
        part_y[n] = (2.0 * dot(low, piece(inner_at((1, dz), 1)), NN)).astype(jnp.bfloat16)
        cross.append(remote(part_y.at[n], land_y.at[n], py_sem, n, "inner", inner_at((1, 0), 1)))
        cross[-1].start()

    row16 = lax.broadcasted_iota(jnp.int32, (rows_n, 128), 0)
    lane16 = lax.broadcasted_iota(jnp.int32, (rows_n, 128), 1)
    num = jnp.sum(gap * masked * masked, axis=1, keepdims=True) + 2.0 * jnp.sum(
        low.astype(jnp.float32) * fitted, axis=1, keepdims=True
    )
    sq = jnp.sum(masked * masked, axis=1, keepdims=True)
    tile = jnp.where(lane16 == row16, num, 0.0) + jnp.where(lane16 == row16 + 16, sq, 0.0)
    e_row = jnp.sum(tile, axis=0, keepdims=True)
    e_send[...] = e_row
    e_copies = start_all(
        [
            remote(e_send, e_land.at[n], e_sem, n, "inner", inner_at(rel, 1))
            for n, rel in enumerate(PEERS)
        ]
    )

    down = []
    for n, dz in enumerate(order):
        own = 2.0 * dot(low, piece(inner_at((0, dz), 1)), NN)
        cross[n].wait_recv()
        own = own + land_y[n].astype(jnp.float32)
        if dz:
            part_z[n] = own.astype(jnp.bfloat16)
            down.append(remote(part_z.at[n], land_z.at[n], pz_sem, n, "inner", inner_at((0, dz), 1)))
            down[-1].start()
    coulomb = own

    own_cols = jnp.transpose(own_xyz)
    for a in range(16):
        if a > 0:
            x_copies[a - 1].wait_recv()
        there = own_xyz if a == 0 else x_land[a - 1]
        r2 = jnp.zeros((128, 128), jnp.float32)
        for k in range(3):
            d = own_cols[:, k : k + 1] - there[k : k + 1, :]
            r2 = r2 + d * d
        hi, lo = split(lax.rsqrt(r2 + 1.0))
        k_hi[:, a * 128 : (a + 1) * 128] = hi
        k_lo[:, a * 128 : (a + 1) * 128] = lo

    for copy in e_copies:
        copy.wait_recv()
    total = e_row
    for n in range(N_IN):
        total = total + e_land[n]
    num = jnp.sum(jnp.where(lane16 == row16, total, 0.0), axis=1, keepdims=True)
    sq = jnp.sum(jnp.where(lane16 == row16 + 16, total, 0.0), axis=1, keepdims=True)
    energy = num / (sq + EPSILON)

    for n in reversed(range(N_Z)):
        down[n].wait_recv()
        coulomb = coulomb + land_z[n].astype(jnp.float32)

    sigma = gap * masked + active * coulomb
    refined = active * (masked - (sigma - energy * masked) / gap)
    refined_ref[...] = refined
    both = dot(refined.astype(jnp.bfloat16), chg_ref[...], NT)
    first = lane16[0:STATES] < 64
    own = jnp.where(first, both[0:STATES], both[STATES:])
    c_send[...] = own
    c_copies = start_all(
        [
            remote(c_send, c_land.at[n], c_sem, n, "inner", inner_at(rel, 1))
            for n, rel in enumerate(PEERS)
        ]
    )
    charges = own
    for n in reversed(range(N_IN)):
        c_copies[n].wait_recv()
        charges = charges + c_land[n]

    g_send[...] = charges
    g_copies = start_all(
        [remote(g_send, g_land.at[a - 1], g_sem, a - 1, "grp", grp_at(a, 1)) for a in range(1, 16)]
    )

    rows = jnp.concatenate([jnp.where(first, charges, 0.0), jnp.where(first, 0.0, charges)], axis=0)
    rows_hi, rows_lo = split(rows)
    with_hi = dot(jnp.concatenate([rows_hi, rows_lo], axis=0), k_hi[...], NN)
    field = with_hi[0:16] + with_hi[16:32] + dot(rows_hi, k_lo[...], NN)

    t = lax.rem(me, STATES)
    half = me // STATES
    in_half = (lax.broadcasted_iota(jnp.int32, (1, 128), 1) // 64) == half
    out_lane = lax.broadcasted_iota(jnp.int32, (16, 16), 1)
    out_row = lax.broadcasted_iota(jnp.int32, (16, 16), 0)
    for copies in ([to_y], to_z, onward, x_copies, cross, e_copies, down, c_copies):
        for c in copies:
            c.wait_send()
    block = jnp.zeros((16, 16), jnp.float32)
    for a in range(16):
        if a > 0:
            g_copies[a - 1].wait_recv()
        src = g_send if a == 0 else g_land.at[a - 1]
        q = jnp.where(in_half, src[pl.ds(t, 1), :], 0.0)
        column = jnp.sum(field[:, a * 128 : (a + 1) * 128] * q, axis=1, keepdims=True)
        block = jnp.where(out_lane == grp_at(a, -1), column, block)
    same = (out_lane == grp) & (out_row // STATES == half)
    block_ref[...] = jnp.where(same, jnp.where(out_row % STATES == t, energy, 0.0), block)
    for c in g_copies:
        c.wait_send()


def hand_over(refined_ref, block_ref, refined_hbm, block_hbm, rows, sems):
    big = pltpu.make_async_copy(refined_ref, refined_hbm, sems.at[0])
    big.start()
    for r in range(block_ref.shape[0]):
        rows[r] = block_ref[r : r + 1, :]
    small = pltpu.make_async_copy(rows, block_hbm, sems.at[1])
    small.start()
    big.wait()
    small.wait()


def local(
    amplitudes, factors, atom_charges, eps_occ, eps_vir, occ_count, vir_count, atom_list, positions
):
    monomers, states, pairs = amplitudes.shape
    aux, every = factors.shape[1:]
    rows = monomers * states
    vmem = pl.BlockSpec(memory_space=pltpu.VMEM)
    hbm = pl.BlockSpec(memory_space=pl.ANY)
    bf, f32, i32 = jnp.bfloat16, jnp.float32, jnp.int32
    by_tile = jnp.transpose(factors, (1, 0, 2)).reshape(aux, monomers, every // 128, 128)
    sem = pltpu.SemaphoreType.DMA
    refined, block = pl.pallas_call(
        kernel,
        name="exciton",
        out_shape=(
            pltpu.VMEM((rows, pairs), f32),
            pltpu.VMEM((rows, rows), f32),
        ),
        in_specs=[hbm] * 9,
        out_specs=(vmem, vmem),
        scratch_shapes=[
            pltpu.VMEM((rows, pairs), bf),
            pltpu.VMEM((monomers * 64, pairs), bf),
            pltpu.SMEM(eps_occ.shape, f32),
            pltpu.VMEM(eps_vir.shape, f32),
            pltpu.SMEM(occ_count.shape, i32),
            pltpu.SMEM(vir_count.shape, i32),
            pltpu.VMEM((1, 128), i32),
            pltpu.VMEM(positions.shape, f32),
            pltpu.VMEM((every // 128, 128, monomers, 128), bf),
            pltpu.VMEM((rows, pairs), bf),
            pltpu.VMEM((N_Z, rows, pairs), bf),
            pltpu.VMEM((N_Z, rows, pairs), bf),
            pltpu.VMEM((Z, rows, pairs), bf),
            pltpu.VMEM((Z, rows, pairs), bf),
            pltpu.VMEM((N_Z, rows, pairs), bf),
            pltpu.VMEM((N_Z, rows, pairs), bf),
            pltpu.VMEM((1, 128), f32),
            pltpu.VMEM((N_IN, 1, 128), f32),
            pltpu.VMEM((8, 128), f32),
            pltpu.VMEM((N_IN, 8, 128), f32),
            pltpu.VMEM((8, 128), f32),
            pltpu.VMEM((N_GRP, 8, 128), f32),
            pltpu.VMEM((8, 128), f32),
            pltpu.VMEM((N_GRP, 8, 128), f32),
            pltpu.VMEM((8, positions.shape[1]), f32),
            pltpu.VMEM((128, 2048), bf),
            pltpu.VMEM((128, 2048), bf),
            sem((8,)),
            sem,
            sem((2, 1)),
            sem((2, N_Z)),
            sem((2, N_Z)),
            sem((2, Z)),
            sem((2, N_Z)),
            sem((2, N_IN)),
            sem((2, N_IN)),
            sem((2, N_GRP)),
            sem((2, N_GRP)),
        ],
        compiler_params=pltpu.CompilerParams(collective_id=0, has_side_effects=True),
    )(
        amplitudes.reshape(rows, pairs),
        by_tile.transpose(0, 2, 1, 3),
        atom_charges.reshape(monomers * 64, pairs),
        eps_occ, eps_vir, occ_count, vir_count, atom_list.reshape(1, -1), positions,
    )
    refined, block = pl.pallas_call(
        hand_over,
        name="hand_over",
        out_shape=(
            jax.ShapeDtypeStruct((rows, pairs), f32),
            jax.ShapeDtypeStruct((rows, 1, rows), f32),
        ),
        in_specs=[vmem, vmem],
        out_specs=(hbm, hbm),
        scratch_shapes=[pltpu.VMEM((rows, 1, rows), f32), sem((2,))],
    )(*(pltpu.with_memory_space_constraint(a, pltpu.VMEM) for a in (refined, block)))
    return refined.reshape(monomers, states, pairs), jnp.swapaxes(block, 1, 2)


def solution(mesh):
    in_specs = (
        P("grp", None, "inner"),
        P("grp", "inner", None),
        P("grp", None, "inner"),
        P("grp", None),
        P("grp", None),
        P("grp"),
        P("grp"),
        P("grp"),
        P(),
    )
    out_specs = (P("grp", None, "inner"), P("grp", None, "inner"))
    return jax.shard_map(local, mesh=mesh, in_specs=in_specs, out_specs=out_specs, check_vma=False)
```

time: 54.5 us -> 45.7 us (0.84)
  Pallas kernels: 51 us -> 45 us
  local copies, waits for them, and re-layouts: 2.72 us -> 0 us
    pallas_call x1 -> x2, Pallas kernels: 51 us -> 45 us  [the longest x1 44.3 us: local(): pl.pallas_call(kernel, name='exciton', out_shape=(pltpu.VMEM((rows, pairs...]
    unnamed x2 -> x0, local copies, waits for them, and re-layouts: 2.72 us -> none
where the time goes in v2:
time: 45.7 us; the launch traced here: 45.6 us
  Pallas kernels  45 us (98%)
  between operations  0.64 us (1%)
    pallas_call x1, Pallas kernels, local(): pl.pallas_call(kernel, name='exciton', out_shape=(pltpu.VMEM((rows, pairs...  44.3 us

profile of v2, /device:TPU:1, one launch (start us, length us, event | category | flops | bytes accessed | tf_op | source)
XLA Modules:
  0.0 45.6 jit_solution(2668430618103820207)
XLA Ops:
  0.6 44.3 %exciton.1 = (f32[16,768]{1,0:T(8,128)S(1)}, f32[16,16]{1,0:T(8,128)S(1)}) custom-call(bf16[16,768]{1,0:T(8,128)(2,1)} %bitcast.14, bf16[125,96,2,128]{3,2,1,0:T(2,128)(2,1)} %bitcast.12, bf16[128,768]{1,0:T(8,128)(2,1)} %bitcast.13, f32[2,48]{1,0:T(2,128)} %occ_e_hbm.1, f32[2,256]{1,0:T(2,128)} %vir_e_hbm.1, s32[2]{0:T(128)} %occ_n_hbm.1, s32[2]{0:T(128)} %vir_n_hbm.1, ...), custom_call_target="tpu_custom_call" | custom-call | tf_op jit(solution)/shard_map/exciton/pallas_call | solution.py:315
  45.0 0.6 %hand_over.1 = (f32[16,768]{1,0:T(8,128)}, f32[16,1,16]{2,1,0:T(1,128)}) custom-call(f32[16,768]{1,0:T(8,128)S(1)} %get-tuple-element.6.refined_ref, f32[16,16]{1,0:T(8,128)S(1)} %get-tuple-element.7.block_ref), custom_call_target="tpu_custom_call" | custom-call | tf_op jit(solution)/shard_map/hand_over/pallas_call | solution.py:371

commit v3 on v2

--- a/solution.py
+++ b/solution.py
@@ -11,12 +11,15 @@
 Z = 8
 MESH = pl.DeviceIdType.MESH
 FAR_Z = (4, 3, 5, 2, 6, 1, 7)
+STRAIGHT = (4, 3, 5)
+SUMMED = (2, 6, 1, 7, 0)
 PEERS = sorted(
     [(dy, dz) for dy in (0, 1) for dz in range(Z) if (dy, dz) != (0, 0)],
     key=lambda r: -(2 * r[0] + min(r[1], Z - r[1])),
 )
 N_IN = len(PEERS)
 N_Z = len(FAR_Z)
+CROWD = [(dy, a) for dy in (1, 0) for a in range(1, 16)]
 N_GRP = 15
 NT = (((1,), (1,)), ((), ()))
 NN = (((1,), (0,)), ((), ()))
@@ -42,12 +45,16 @@
 
 
 def remote(src, dst, sems, n, axis, where):
+    return remote_to(src, dst, sems, n, {axis: where})
+
+
+def remote_to(src, dst, sems, n, device):
     return pltpu.make_async_remote_copy(
         src_ref=src,
         dst_ref=dst,
         send_sem=sems.at[0, n],
         recv_sem=sems.at[1, n],
-        device_id={axis: where},
+        device_id=device,
         device_id_type=MESH,
     )
 
@@ -62,9 +69,9 @@
     amp_hbm, fac_hbm, chg_hbm, occ_e_hbm, vir_e_hbm, occ_n_hbm, vir_n_hbm, atoms_hbm, pos_hbm,
     refined_ref, block_ref,
     amp_ref, chg_ref, occ_e, vir_e, occ_n, vir_n, atoms_ref, pos_ref,
-    fac, amp_y, amp_z, amp_yz, part_y, land_y, part_z, land_z,
-    e_send, e_land, c_send, c_land, g_send, g_land, x_send, x_land, pos8, k_hi, k_lo,
-    in_sem, fac_sem, ay_sem, az_sem, ayz_sem, py_sem, pz_sem, e_sem, c_sem, g_sem, x_sem,
+    fac, amp_y, amp_z, amp_yz, part_s, land_s, part_y, land_y, part_z, land_z,
+    e_send, e_land, c_send, c_land, g_send, g_row, p_land, g_land, x_send, x_land, pos8, k_hi, k_lo,
+    in_sem, fac_sem, ay_sem, az_sem, ayz_sem, ps_sem, py_sem, pz_sem, e_sem, c_sem, p_sem, g_sem, x_sem,
 ):
     me = lax.axis_index("inner")
     grp = lax.axis_index("grp")
@@ -85,54 +92,27 @@
     inputs = start_all(
         [pltpu.make_async_copy(src, dst, in_sem.at[n]) for n, (src, dst) in enumerate(pairs_in)]
     )
-    inputs[0].wait()
-    pl.semaphore_wait(barrier, 1 + N_Z + N_GRP)
-
-    to_y = remote(amp_ref, amp_y, ay_sem, 0, "inner", inner_at((1, 0), 1))
-    to_y.start()
-    to_z = start_all(
-        [
-            remote(amp_ref, amp_z.at[n], az_sem, n, "inner", inner_at((0, dz), 1))
-            for n, dz in enumerate(FAR_Z)
-        ]
-    )
     loads = []
     for j in range(tiles):
         loads.append(pltpu.make_async_copy(fac_hbm.at[:, j], fac.at[j, pl.ds(0, aux)], fac_sem))
         loads[-1].start()
-    to_y.wait_recv()
-    onward = start_all(
-        [
-            remote(amp_y, amp_yz.at[n], ayz_sem, n, "inner", inner_at((0, dz), 1))
-            for n, dz in enumerate(FAR_Z)
-        ]
-    )
-    for copy in inputs[1:]:
+    for copy in inputs:
         copy.wait()
-    for j in range(tiles):
-        fac[j, aux:128] = jnp.zeros((128 - aux, 2, 128), jnp.bfloat16)
-    flat = fac.reshape(tiles, 256, 128)
-
-    def piece(who):
-        return jnp.concatenate([flat[who * per + m] for m in range(per)], axis=1)
 
     pos8[...] = jnp.zeros_like(pos8)
     pos8[0:3, :] = pos_ref[...]
     p_all = pos8[...]
-    p_hi = p_all.astype(jnp.bfloat16)
-    rest = p_all - p_hi.astype(jnp.float32)
-    p_mid = rest.astype(jnp.bfloat16)
-    p_lo = (rest - p_mid.astype(jnp.float32)).astype(jnp.bfloat16)
+    p_hi = p_all.astype(jnp.bfloat16).astype(jnp.float32)
+    p_mid = (p_all - p_hi).astype(jnp.bfloat16).astype(jnp.float32)
+    p_lo = p_all - p_hi - p_mid
     hot = (
         (lax.broadcasted_iota(jnp.int32, (pos_ref.shape[1], 128), 0) == atoms_ref[...])
         .astype(jnp.float32)
         .astype(jnp.bfloat16)
     )
-    own_xyz = dot(p_hi, hot, NN) + dot(p_mid, hot, NN) + dot(p_lo, hot, NN)
+    xyz3 = dot(jnp.concatenate([p_hi, p_mid, p_lo], axis=0).astype(jnp.bfloat16), hot, NN)
+    own_xyz = xyz3[0:8] + xyz3[8:16] + xyz3[16:24]
     x_send[...] = own_xyz
-    x_copies = start_all(
-        [remote(x_send, x_land.at[a - 1], x_sem, a - 1, "grp", grp_at(a, 1)) for a in range(1, 16)]
-    )
 
     lane = lax.broadcasted_iota(jnp.int32, (STATES, pairs), 1)
     seg, vir = lane // NVIR, lane % NVIR
@@ -159,7 +139,27 @@
         axis=0,
     )
     masked = amp_ref[...].astype(jnp.float32) * active
-
+    own_num = jnp.sum(gap * masked * masked, axis=1, keepdims=True)
+    own_sq = jnp.sum(masked * masked, axis=1, keepdims=True)
+    for j in range(tiles):
+        fac[j, aux:128] = jnp.zeros((128 - aux, 2, 128), jnp.bfloat16)
+    flat = fac.reshape(tiles, 256, 128)
+
+    def piece(who):
+        return jnp.concatenate([flat[who * per + m] for m in range(per)], axis=1)
+
+    pl.semaphore_wait(barrier, 1 + N_Z + N_GRP)
+    to_y = remote(amp_ref, amp_y, ay_sem, 0, "inner", inner_at((1, 0), 1))
+    to_y.start()
+    to_z = start_all(
+        [
+            remote(amp_ref, amp_z.at[n], az_sem, n, "inner", inner_at((0, dz), 1))
+            for n, dz in enumerate(FAR_Z)
+        ]
+    )
+    x_copies = start_all(
+        [remote(x_send, x_land.at[a - 1], x_sem, a - 1, "grp", grp_at(a, 1)) for a in range(1, 16)]
+    )
     for c in loads:
         c.wait()
 
@@ -168,10 +168,19 @@
         return dot(theirs, piece(who), NT)
 
     fitted = dot(masked.astype(jnp.bfloat16), piece(me), NT)
-    fitted = fitted + fit(amp_y[...], inner_at((1, 0), 1))
+    onward = []
     for n in reversed(range(N_Z)):
         to_z[n].wait_recv()
         fitted = fitted + fit(amp_z[n], inner_at((0, FAR_Z[n]), -1))
+        if n == N_Z - 2:
+            to_y.wait_recv()
+            onward = start_all(
+                [
+                    remote(amp_y, amp_yz.at[m], ayz_sem, m, "inner", inner_at((0, dz), 1))
+                    for m, dz in enumerate(FAR_Z)
+                ]
+            )
+            fitted = fitted + fit(amp_y[...], inner_at((1, 0), 1))
     for n in reversed(range(N_Z)):
         onward[n].wait_recv()
         fitted = fitted + fit(amp_yz[n], inner_at((1, FAR_Z[n]), -1))
@@ -180,20 +189,36 @@
     fitted = jnp.where(parity == monomer, fitted, 0.0)
     low = fitted.astype(jnp.bfloat16)
 
-    order = FAR_Z + (0,)
-    cross = []
-    for n, dz in enumerate(order):
-        part_y[n] = (2.0 * dot(low, piece(inner_at((1, dz), 1)), NN)).astype(jnp.bfloat16)
-        cross.append(remote(part_y.at[n], land_y.at[n], py_sem, n, "inner", inner_at((1, 0), 1)))
-        cross[-1].start()
+    def partial_to(rel):
+        return 2.0 * dot(low, piece(inner_at(rel, 1)), NN)
+
+    straight, cross, down = {}, {}, {}
+
+    def send_straight(n):
+        rel = (1, STRAIGHT[n])
+        part_s[n] = partial_to(rel).astype(jnp.bfloat16)
+        straight[n] = remote(part_s.at[n], land_s.at[n], ps_sem, n, "inner", inner_at(rel, 1))
+        straight[n].start()
+
+    def send_cross(n):
+        part_y[n] = partial_to((1, SUMMED[n])).astype(jnp.bfloat16)
+        cross[n] = remote(part_y.at[n], land_y.at[n], py_sem, n, "inner", inner_at((1, 0), 1))
+        cross[n].start()
+
+    def send_down(n, value):
+        rel = (0, FAR_Z[n])
+        part_z[n] = value.astype(jnp.bfloat16)
+        down[n] = remote(part_z.at[n], land_z.at[n], pz_sem, n, "inner", inner_at(rel, 1))
+        down[n].start()
+
+    send_straight(0)
+    send_cross(0)
+    send_cross(1)
 
     row16 = lax.broadcasted_iota(jnp.int32, (rows_n, 128), 0)
     lane16 = lax.broadcasted_iota(jnp.int32, (rows_n, 128), 1)
-    num = jnp.sum(gap * masked * masked, axis=1, keepdims=True) + 2.0 * jnp.sum(
-        low.astype(jnp.float32) * fitted, axis=1, keepdims=True
-    )
-    sq = jnp.sum(masked * masked, axis=1, keepdims=True)
-    tile = jnp.where(lane16 == row16, num, 0.0) + jnp.where(lane16 == row16 + 16, sq, 0.0)
+    num = own_num + 2.0 * jnp.sum(low.astype(jnp.float32) * fitted, axis=1, keepdims=True)
+    tile = jnp.where(lane16 == row16, num, 0.0) + jnp.where(lane16 == row16 + 16, own_sq, 0.0)
     e_row = jnp.sum(tile, axis=0, keepdims=True)
     e_send[...] = e_row
     e_copies = start_all(
@@ -202,16 +227,19 @@
             for n, rel in enumerate(PEERS)
         ]
     )
-
-    down = []
-    for n, dz in enumerate(order):
-        own = 2.0 * dot(low, piece(inner_at((0, dz), 1)), NN)
+    send_straight(1)
+    send_straight(2)
+    send_cross(2)
+    send_cross(3)
+    for n in range(3):
+        send_down(n, partial_to((0, FAR_Z[n])))
+    send_cross(4)
+    for n, dz in enumerate(SUMMED):
+        own = partial_to((0, dz))
         cross[n].wait_recv()
         own = own + land_y[n].astype(jnp.float32)
         if dz:
-            part_z[n] = own.astype(jnp.bfloat16)
-            down.append(remote(part_z.at[n], land_z.at[n], pz_sem, n, "inner", inner_at((0, dz), 1)))
-            down[-1].start()
+            send_down(n + 3, own)
     coulomb = own
 
     own_cols = jnp.transpose(own_xyz)
@@ -236,6 +264,9 @@
     sq = jnp.sum(jnp.where(lane16 == row16 + 16, total, 0.0), axis=1, keepdims=True)
     energy = num / (sq + EPSILON)
 
+    for n in range(3):
+        straight[n].wait_recv()
+        coulomb = coulomb + land_s[n].astype(jnp.float32)
     for n in reversed(range(N_Z)):
         down[n].wait_recv()
         coulomb = coulomb + land_z[n].astype(jnp.float32)
@@ -249,19 +280,30 @@
     c_send[...] = own
     c_copies = start_all(
         [
-            remote(c_send, c_land.at[n], c_sem, n, "inner", inner_at(rel, 1))
-            for n, rel in enumerate(PEERS)
+            remote(c_send, c_land.at[n], c_sem, n, "inner", inner_at((0, dz), 1))
+            for n, dz in enumerate(FAR_Z)
         ]
     )
     charges = own
-    for n in reversed(range(N_IN)):
+    for n in reversed(range(N_Z)):
         c_copies[n].wait_recv()
         charges = charges + c_land[n]
-
     g_send[...] = charges
+    g_row[...] = g_send[pl.ds(lax.rem(me, STATES), 1), :]
+    p_copy = remote(g_send, p_land, p_sem, 0, "inner", inner_at((1, 0), 1))
+    p_copy.start()
     g_copies = start_all(
-        [remote(g_send, g_land.at[a - 1], g_sem, a - 1, "grp", grp_at(a, 1)) for a in range(1, 16)]
-    )
+        [
+            remote_to(
+                g_row, g_land.at[n], g_sem, n,
+                {"grp": grp_at(a, 1), "inner": inner_at((dy, 0), 1)},
+            )
+            for n, (dy, a) in enumerate(CROWD)
+        ]
+    )
+    p_copy.wait_recv()
+    p_row = p_land[pl.ds(lax.rem(me, STATES), 1), :]
+    charges = charges + p_land[...]
 
     rows = jnp.concatenate([jnp.where(first, charges, 0.0), jnp.where(first, 0.0, charges)], axis=0)
     rows_hi, rows_lo = split(rows)
@@ -273,15 +315,19 @@
     in_half = (lax.broadcasted_iota(jnp.int32, (1, 128), 1) // 64) == half
     out_lane = lax.broadcasted_iota(jnp.int32, (16, 16), 1)
     out_row = lax.broadcasted_iota(jnp.int32, (16, 16), 0)
-    for copies in ([to_y], to_z, onward, x_copies, cross, e_copies, down, c_copies):
+    for copies in ([to_y], to_z, onward, x_copies, straight.values(), cross.values(), e_copies, down.values(), c_copies):
         for c in copies:
             c.wait_send()
+    p_copy.wait_send()
     block = jnp.zeros((16, 16), jnp.float32)
     for a in range(16):
         if a > 0:
             g_copies[a - 1].wait_recv()
-        src = g_send if a == 0 else g_land.at[a - 1]
-        q = jnp.where(in_half, src[pl.ds(t, 1), :], 0.0)
+            g_copies[a - 1 + N_GRP].wait_recv()
+            q = g_land[a - 1] + g_land[a - 1 + N_GRP]
+        else:
+            q = g_row[...] + p_row
+        q = jnp.where(in_half, q, 0.0)
         column = jnp.sum(field[:, a * 128 : (a + 1) * 128] * q, axis=1, keepdims=True)
         block = jnp.where(out_lane == grp_at(a, -1), column, block)
     same = (out_lane == grp) & (out_row // STATES == half)
@@ -334,16 +380,20 @@
             pltpu.VMEM((rows, pairs), bf),
             pltpu.VMEM((N_Z, rows, pairs), bf),
             pltpu.VMEM((N_Z, rows, pairs), bf),
-            pltpu.VMEM((Z, rows, pairs), bf),
-            pltpu.VMEM((Z, rows, pairs), bf),
+            pltpu.VMEM((3, rows, pairs), bf),
+            pltpu.VMEM((3, rows, pairs), bf),
+            pltpu.VMEM((5, rows, pairs), bf),
+            pltpu.VMEM((5, rows, pairs), bf),
             pltpu.VMEM((N_Z, rows, pairs), bf),
             pltpu.VMEM((N_Z, rows, pairs), bf),
             pltpu.VMEM((1, 128), f32),
             pltpu.VMEM((N_IN, 1, 128), f32),
             pltpu.VMEM((8, 128), f32),
-            pltpu.VMEM((N_IN, 8, 128), f32),
+            pltpu.VMEM((N_Z, 8, 128), f32),
             pltpu.VMEM((8, 128), f32),
-            pltpu.VMEM((N_GRP, 8, 128), f32),
+            pltpu.VMEM((1, 128), f32),
+            pltpu.VMEM((8, 128), f32),
+            pltpu.VMEM((2 * N_GRP, 1, 128), f32),
             pltpu.VMEM((8, 128), f32),
             pltpu.VMEM((N_GRP, 8, 128), f32),
             pltpu.VMEM((8, positions.shape[1]), f32),
@@ -354,11 +404,13 @@
             sem((2, 1)),
             sem((2, N_Z)),
             sem((2, N_Z)),
-            sem((2, Z)),
+            sem((2, 3)),
+            sem((2, 5)),
             sem((2, N_Z)),
             sem((2, N_IN)),
-            sem((2, N_IN)),
-            sem((2, N_GRP)),
+            sem((2, N_Z)),
+            sem((2, 1)),
+            sem((2, 2 * N_GRP)),
             sem((2, N_GRP)),
         ],
         compiler_params=pltpu.CompilerParams(collective_id=0, has_side_effects=True),

time: 45.7 us -> 48.6 us (1.063)
  Pallas kernels: 45 us -> 47.9 us
    pallas_call x1, Pallas kernels: 44.3 us -> 47.2 us  [local(): pl.pallas_call(kernel, name='exciton', out_shape=(pltpu.VMEM((rows, pairs...]
where the time goes in v3:
time: 48.6 us; the launch traced here: 48.5 us
  Pallas kernels  47.9 us (99%)
  between operations  0.64 us (1%)
    pallas_call x1, Pallas kernels, local(): pl.pallas_call(kernel, name='exciton', out_shape=(pltpu.VMEM((rows, pairs...  47.2 us

profile of v3, /device:TPU:1, one launch (start us, length us, event | category | flops | bytes accessed | tf_op | source)
XLA Modules:
  0.0 48.5 jit_solution(655286272379766353)
XLA Ops:
  0.6 47.2 %exciton.1 = (f32[16,768]{1,0:T(8,128)S(1)}, f32[16,16]{1,0:T(8,128)S(1)}) custom-call(bf16[16,768]{1,0:T(8,128)(2,1)} %bitcast.14, bf16[125,96,2,128]{3,2,1,0:T(2,128)(2,1)} %bitcast.12, bf16[128,768]{1,0:T(8,128)(2,1)} %bitcast.13, f32[2,48]{1,0:T(2,128)} %occ_e_hbm.1, f32[2,256]{1,0:T(2,128)} %vir_e_hbm.1, s32[2]{0:T(128)} %occ_n_hbm.1, s32[2]{0:T(128)} %vir_n_hbm.1, ...), custom_call_target="tpu_custom_call" | custom-call | tf_op jit(solution)/shard_map/exciton/pallas_call | solution.py:361
  47.9 0.6 %hand_over.1 = (f32[16,768]{1,0:T(8,128)}, f32[16,1,16]{2,1,0:T(1,128)}) custom-call(f32[16,768]{1,0:T(8,128)S(1)} %get-tuple-element.6.refined_ref, f32[16,16]{1,0:T(8,128)S(1)} %get-tuple-element.7.block_ref), custom_call_target="tpu_custom_call" | custom-call | tf_op jit(solution)/shard_map/hand_over/pallas_call | solution.py:423

commit v4 on v3

--- a/solution.py
+++ b/solution.py
@@ -11,8 +11,9 @@
 Z = 8
 MESH = pl.DeviceIdType.MESH
 FAR_Z = (4, 3, 5, 2, 6, 1, 7)
-STRAIGHT = (4, 3, 5)
-SUMMED = (2, 6, 1, 7, 0)
+NEAR_Z = (1, 7, 2, 6)
+RELAYED = ((1, 2, 3), (7, 6, 5), (2, 2, 4))
+ARRIVALS = (1, 7, 2, 6, 3, 5, 4)
 PEERS = sorted(
     [(dy, dz) for dy in (0, 1) for dz in range(Z) if (dy, dz) != (0, 0)],
     key=lambda r: -(2 * r[0] + min(r[1], Z - r[1])),
@@ -69,9 +70,9 @@
     amp_hbm, fac_hbm, chg_hbm, occ_e_hbm, vir_e_hbm, occ_n_hbm, vir_n_hbm, atoms_hbm, pos_hbm,
     refined_ref, block_ref,
     amp_ref, chg_ref, occ_e, vir_e, occ_n, vir_n, atoms_ref, pos_ref,
-    fac, amp_y, amp_z, amp_yz, part_s, land_s, part_y, land_y, part_z, land_z,
+    fac, amp_z, amp_yz, part_y, land_y, part_z, land_z,
     e_send, e_land, c_send, c_land, g_send, g_row, p_land, g_land, x_send, x_land, pos8, k_hi, k_lo,
-    in_sem, fac_sem, ay_sem, az_sem, ayz_sem, ps_sem, py_sem, pz_sem, e_sem, c_sem, p_sem, g_sem, x_sem,
+    in_sem, fac_sem, az_sem, ayz_sem, py_sem, pz_sem, e_sem, c_sem, p_sem, g_sem, x_sem,
 ):
     me = lax.axis_index("inner")
     grp = lax.axis_index("grp")
@@ -81,7 +82,7 @@
     per = pairs // 128
 
     barrier = pltpu.get_barrier_semaphore()
-    for rel in [(1, 0)] + [(0, dz) for dz in FAR_Z]:
+    for rel in [(1, 0)] + [(0, dz) for dz in NEAR_Z]:
         pl.semaphore_signal(barrier, inc=1, device_id={"inner": inner_at(rel, 1)}, device_id_type=MESH)
     for a in range(1, 16):
         pl.semaphore_signal(barrier, inc=1, device_id={"grp": grp_at(a, 1)}, device_id_type=MESH)
@@ -92,11 +93,29 @@
     inputs = start_all(
         [pltpu.make_async_copy(src, dst, in_sem.at[n]) for n, (src, dst) in enumerate(pairs_in)]
     )
+    inputs[0].wait()
+    pl.semaphore_wait(barrier, 1 + len(NEAR_Z) + N_GRP)
+
+    along, across = {}, {}
+
+    def send_along(src, dz, at):
+        n = ARRIVALS.index(at)
+        along[at] = remote(src, amp_z.at[n], az_sem, n, "inner", inner_at((0, dz), 1))
+        along[at].start()
+
+    def send_across(src, at):
+        n = ARRIVALS.index(at) + 1 if at else 0
+        across[at] = remote(src, amp_yz.at[n], ayz_sem, n, "inner", inner_at((1, 0), 1))
+        across[at].start()
+
+    send_across(amp_ref, 0)
+    for dz in NEAR_Z:
+        send_along(amp_ref, dz, dz)
     loads = []
     for j in range(tiles):
         loads.append(pltpu.make_async_copy(fac_hbm.at[:, j], fac.at[j, pl.ds(0, aux)], fac_sem))
         loads[-1].start()
-    for copy in inputs:
+    for copy in inputs[1:]:
         copy.wait()
 
     pos8[...] = jnp.zeros_like(pos8)
@@ -114,6 +133,16 @@
     own_xyz = xyz3[0:8] + xyz3[8:16] + xyz3[16:24]
     x_send[...] = own_xyz
 
+    for at, step, then in RELAYED:
+        along[at].wait_recv()
+        shard = amp_z.at[ARRIVALS.index(at)]
+        send_along(shard, step, then)
+        send_across(shard, at)
+    along[6].wait_recv()
+    send_across(amp_z.at[ARRIVALS.index(6)], 6)
+    x_copies = start_all(
+        [remote(x_send, x_land.at[a - 1], x_sem, a - 1, "grp", grp_at(a, 1)) for a in range(1, 16)]
+    )
     lane = lax.broadcasted_iota(jnp.int32, (STATES, pairs), 1)
     seg, vir = lane // NVIR, lane % NVIR
     vir_in = [vir < vir_n[c] for c in range(2)]
@@ -148,18 +177,6 @@
     def piece(who):
         return jnp.concatenate([flat[who * per + m] for m in range(per)], axis=1)
 
-    pl.semaphore_wait(barrier, 1 + N_Z + N_GRP)
-    to_y = remote(amp_ref, amp_y, ay_sem, 0, "inner", inner_at((1, 0), 1))
-    to_y.start()
-    to_z = start_all(
-        [
-            remote(amp_ref, amp_z.at[n], az_sem, n, "inner", inner_at((0, dz), 1))
-            for n, dz in enumerate(FAR_Z)
-        ]
-    )
-    x_copies = start_all(
-        [remote(x_send, x_land.at[a - 1], x_sem, a - 1, "grp", grp_at(a, 1)) for a in range(1, 16)]
-    )
     for c in loads:
         c.wait()
 
@@ -167,53 +184,32 @@
         theirs = (amps.astype(jnp.float32) * active_of(who)).astype(jnp.bfloat16)
         return dot(theirs, piece(who), NT)
 
-    fitted = dot(masked.astype(jnp.bfloat16), piece(me), NT)
-    onward = []
-    for n in reversed(range(N_Z)):
-        to_z[n].wait_recv()
-        fitted = fitted + fit(amp_z[n], inner_at((0, FAR_Z[n]), -1))
-        if n == N_Z - 2:
-            to_y.wait_recv()
-            onward = start_all(
-                [
-                    remote(amp_y, amp_yz.at[m], ayz_sem, m, "inner", inner_at((0, dz), 1))
-                    for m, dz in enumerate(FAR_Z)
-                ]
-            )
-            fitted = fitted + fit(amp_y[...], inner_at((1, 0), 1))
-    for n in reversed(range(N_Z)):
-        onward[n].wait_recv()
-        fitted = fitted + fit(amp_yz[n], inner_at((1, FAR_Z[n]), -1))
+    def fit_along(at):
+        return fit(amp_z[ARRIVALS.index(at)], inner_at((0, at), -1))
+
+    def fit_across(at):
+        across[at].wait_recv()
+        return fit(amp_yz[ARRIVALS.index(at) + 1 if at else 0], inner_at((1, at), -1))
+
+    fitted = dot(masked.astype(jnp.bfloat16), piece(me), NT) + fit_along(1) + fit_along(7)
+    for at in (3, 5, 4):
+        along[at].wait_recv()
+        send_across(amp_z.at[ARRIVALS.index(at)], at)
+    for at in (2, 6, 3, 5, 4):
+        fitted = fitted + fit_along(at)
+    for at in (0,) + ARRIVALS:
+        fitted = fitted + fit_across(at)
     parity = lax.broadcasted_iota(jnp.int32, fitted.shape, 1) % 2
     monomer = lax.broadcasted_iota(jnp.int32, fitted.shape, 0) // STATES
     fitted = jnp.where(parity == monomer, fitted, 0.0)
     low = fitted.astype(jnp.bfloat16)
 
-    def partial_to(rel):
-        return 2.0 * dot(low, piece(inner_at(rel, 1)), NN)
-
-    straight, cross, down = {}, {}, {}
-
-    def send_straight(n):
-        rel = (1, STRAIGHT[n])
-        part_s[n] = partial_to(rel).astype(jnp.bfloat16)
-        straight[n] = remote(part_s.at[n], land_s.at[n], ps_sem, n, "inner", inner_at(rel, 1))
-        straight[n].start()
-
-    def send_cross(n):
-        part_y[n] = partial_to((1, SUMMED[n])).astype(jnp.bfloat16)
-        cross[n] = remote(part_y.at[n], land_y.at[n], py_sem, n, "inner", inner_at((1, 0), 1))
-        cross[n].start()
-
-    def send_down(n, value):
-        rel = (0, FAR_Z[n])
-        part_z[n] = value.astype(jnp.bfloat16)
-        down[n] = remote(part_z.at[n], land_z.at[n], pz_sem, n, "inner", inner_at(rel, 1))
-        down[n].start()
-
-    send_straight(0)
-    send_cross(0)
-    send_cross(1)
+    order = FAR_Z + (0,)
+    cross = []
+    for n, dz in enumerate(order):
+        part_y[n] = (2.0 * dot(low, piece(inner_at((1, dz), 1)), NN)).astype(jnp.bfloat16)
+        cross.append(remote(part_y.at[n], land_y.at[n], py_sem, n, "inner", inner_at((1, 0), 1)))
+        cross[-1].start()
 
     row16 = lax.broadcasted_iota(jnp.int32, (rows_n, 128), 0)
     lane16 = lax.broadcasted_iota(jnp.int32, (rows_n, 128), 1)
@@ -227,19 +223,16 @@
             for n, rel in enumerate(PEERS)
         ]
     )
-    send_straight(1)
-    send_straight(2)
-    send_cross(2)
-    send_cross(3)
-    for n in range(3):
-        send_down(n, partial_to((0, FAR_Z[n])))
-    send_cross(4)
-    for n, dz in enumerate(SUMMED):
-        own = partial_to((0, dz))
+
+    down = []
+    for n, dz in enumerate(order):
+        own = 2.0 * dot(low, piece(inner_at((0, dz), 1)), NN)
         cross[n].wait_recv()
         own = own + land_y[n].astype(jnp.float32)
         if dz:
-            send_down(n + 3, own)
+            part_z[n] = own.astype(jnp.bfloat16)
+            down.append(remote(part_z.at[n], land_z.at[n], pz_sem, n, "inner", inner_at((0, dz), 1)))
+            down[-1].start()
     coulomb = own
 
     own_cols = jnp.transpose(own_xyz)
@@ -264,9 +257,6 @@
     sq = jnp.sum(jnp.where(lane16 == row16 + 16, total, 0.0), axis=1, keepdims=True)
     energy = num / (sq + EPSILON)
 
-    for n in range(3):
-        straight[n].wait_recv()
-        coulomb = coulomb + land_s[n].astype(jnp.float32)
     for n in reversed(range(N_Z)):
         down[n].wait_recv()
         coulomb = coulomb + land_z[n].astype(jnp.float32)
@@ -315,7 +305,7 @@
     in_half = (lax.broadcasted_iota(jnp.int32, (1, 128), 1) // 64) == half
     out_lane = lax.broadcasted_iota(jnp.int32, (16, 16), 1)
     out_row = lax.broadcasted_iota(jnp.int32, (16, 16), 0)
-    for copies in ([to_y], to_z, onward, x_copies, straight.values(), cross.values(), e_copies, down.values(), c_copies):
+    for copies in (along.values(), across.values(), x_copies, cross, e_copies, down, c_copies):
         for c in copies:
             c.wait_send()
     p_copy.wait_send()
@@ -377,13 +367,10 @@
             pltpu.VMEM((1, 128), i32),
             pltpu.VMEM(positions.shape, f32),
             pltpu.VMEM((every // 128, 128, monomers, 128), bf),
-            pltpu.VMEM((rows, pairs), bf),
             pltpu.VMEM((N_Z, rows, pairs), bf),
-            pltpu.VMEM((N_Z, rows, pairs), bf),
-            pltpu.VMEM((3, rows, pairs), bf),
-            pltpu.VMEM((3, rows, pairs), bf),
-            pltpu.VMEM((5, rows, pairs), bf),
-            pltpu.VMEM((5, rows, pairs), bf),
+            pltpu.VMEM((Z, rows, pairs), bf),
+            pltpu.VMEM((Z, rows, pairs), bf),
+            pltpu.VMEM((Z, rows, pairs), bf),
             pltpu.VMEM((N_Z, rows, pairs), bf),
             pltpu.VMEM((N_Z, rows, pairs), bf),
             pltpu.VMEM((1, 128), f32),
@@ -401,11 +388,9 @@
             pltpu.VMEM((128, 2048), bf),
             sem((8,)),
             sem,
-            sem((2, 1)),
             sem((2, N_Z)),
-            sem((2, N_Z)),
-            sem((2, 3)),
-            sem((2, 5)),
+            sem((2, Z)),
+            sem((2, Z)),
             sem((2, N_Z)),
             sem((2, N_IN)),
             sem((2, N_Z)),

time: 48.6 us -> 45.2 us (0.930)
  Pallas kernels: 47.9 us -> 44.5 us
    pallas_call x1, Pallas kernels: 47.2 us -> 43.8 us  [local(): pl.pallas_call(kernel, name='exciton', out_shape=(pltpu.VMEM((rows, pairs...]
where the time goes in v4:
time: 45.2 us; the launch traced here: 45.1 us
  Pallas kernels  44.5 us (98%)
  between operations  0.64 us (1%)
    pallas_call x1, Pallas kernels, local(): pl.pallas_call(kernel, name='exciton', out_shape=(pltpu.VMEM((rows, pairs...  43.8 us

profile of v4, /device:TPU:1, one launch (start us, length us, event | category | flops | bytes accessed | tf_op | source)
XLA Modules:
  0.0 45.1 jit_solution(5629059192013694977)
XLA Ops:
  0.6 43.8 %exciton.1 = (f32[16,768]{1,0:T(8,128)S(1)}, f32[16,16]{1,0:T(8,128)S(1)}) custom-call(bf16[16,768]{1,0:T(8,128)(2,1)} %bitcast.14, bf16[125,96,2,128]{3,2,1,0:T(2,128)(2,1)} %bitcast.12, bf16[128,768]{1,0:T(8,128)(2,1)} %bitcast.13, f32[2,48]{1,0:T(2,128)} %occ_e_hbm.1, f32[2,256]{1,0:T(2,128)} %vir_e_hbm.1, s32[2]{0:T(128)} %occ_n_hbm.1, s32[2]{0:T(128)} %vir_n_hbm.1, ...), custom_call_target="tpu_custom_call" | custom-call | tf_op jit(solution)/shard_map/exciton/pallas_call | solution.py:351
  44.5 0.6 %hand_over.1 = (f32[16,768]{1,0:T(8,128)}, f32[16,1,16]{2,1,0:T(1,128)}) custom-call(f32[16,768]{1,0:T(8,128)S(1)} %get-tuple-element.6.refined_ref, f32[16,16]{1,0:T(8,128)S(1)} %get-tuple-element.7.block_ref), custom_call_target="tpu_custom_call" | custom-call | tf_op jit(solution)/shard_map/hand_over/pallas_call | solution.py:408

commit v5 on v4

--- a/solution.py
+++ b/solution.py
@@ -11,8 +11,6 @@
 Z = 8
 MESH = pl.DeviceIdType.MESH
 FAR_Z = (4, 3, 5, 2, 6, 1, 7)
-NEAR_Z = (1, 7, 2, 6)
-RELAYED = ((1, 2, 3), (7, 6, 5), (2, 2, 4))
 ARRIVALS = (1, 7, 2, 6, 3, 5, 4)
 PEERS = sorted(
     [(dy, dz) for dy in (0, 1) for dz in range(Z) if (dy, dz) != (0, 0)],
@@ -82,7 +80,7 @@
     per = pairs // 128
 
     barrier = pltpu.get_barrier_semaphore()
-    for rel in [(1, 0)] + [(0, dz) for dz in NEAR_Z]:
+    for rel in [(1, 0)] + [(0, dz) for dz in FAR_Z]:
         pl.semaphore_signal(barrier, inc=1, device_id={"inner": inner_at(rel, 1)}, device_id_type=MESH)
     for a in range(1, 16):
         pl.semaphore_signal(barrier, inc=1, device_id={"grp": grp_at(a, 1)}, device_id_type=MESH)
@@ -94,7 +92,7 @@
         [pltpu.make_async_copy(src, dst, in_sem.at[n]) for n, (src, dst) in enumerate(pairs_in)]
     )
     inputs[0].wait()
-    pl.semaphore_wait(barrier, 1 + len(NEAR_Z) + N_GRP)
+    pl.semaphore_wait(barrier, 1 + len(FAR_Z) + N_GRP)
 
     along, across = {}, {}
 
@@ -109,7 +107,7 @@
         across[at].start()
 
     send_across(amp_ref, 0)
-    for dz in NEAR_Z:
+    for dz in FAR_Z:
         send_along(amp_ref, dz, dz)
     loads = []
     for j in range(tiles):
@@ -133,13 +131,9 @@
     own_xyz = xyz3[0:8] + xyz3[8:16] + xyz3[16:24]
     x_send[...] = own_xyz
 
-    for at, step, then in RELAYED:
+    for at in (1, 7, 2, 6):
         along[at].wait_recv()
-        shard = amp_z.at[ARRIVALS.index(at)]
-        send_along(shard, step, then)
-        send_across(shard, at)
-    along[6].wait_recv()
-    send_across(amp_z.at[ARRIVALS.index(6)], 6)
+        send_across(amp_z.at[ARRIVALS.index(at)], at)
     x_copies = start_all(
         [remote(x_send, x_land.at[a - 1], x_sem, a - 1, "grp", grp_at(a, 1)) for a in range(1, 16)]
     )

time: 45.2 us -> 46.2 us (1.022)
  Pallas kernels: 44.5 us -> 45.4 us
    pallas_call x1, Pallas kernels: 43.8 us -> 44.8 us  [local(): pl.pallas_call(kernel, name='exciton', out_shape=(pltpu.VMEM((rows, pairs...]
where the time goes in v5:
time: 46.2 us; the launch traced here: 46.1 us
  Pallas kernels  45.4 us (98%)
  between operations  0.64 us (1%)
    pallas_call x1, Pallas kernels, local(): pl.pallas_call(kernel, name='exciton', out_shape=(pltpu.VMEM((rows, pairs...  44.8 us

profile of v5, /device:TPU:1, one launch (start us, length us, event | category | flops | bytes accessed | tf_op | source)
XLA Modules:
  0.0 46.1 jit_solution(13528414062964014533)
XLA Ops:
  0.6 44.8 %exciton.1 = (f32[16,768]{1,0:T(8,128)S(1)}, f32[16,16]{1,0:T(8,128)S(1)}) custom-call(bf16[16,768]{1,0:T(8,128)(2,1)} %bitcast.14, bf16[125,96,2,128]{3,2,1,0:T(2,128)(2,1)} %bitcast.12, bf16[128,768]{1,0:T(8,128)(2,1)} %bitcast.13, f32[2,48]{1,0:T(2,128)} %occ_e_hbm.1, f32[2,256]{1,0:T(2,128)} %vir_e_hbm.1, s32[2]{0:T(128)} %occ_n_hbm.1, s32[2]{0:T(128)} %vir_n_hbm.1, ...), custom_call_target="tpu_custom_call" | custom-call | tf_op jit(solution)/shard_map/exciton/pallas_call | solution.py:345
  45.4 0.6 %hand_over.1 = (f32[16,768]{1,0:T(8,128)}, f32[16,1,16]{2,1,0:T(1,128)}) custom-call(f32[16,768]{1,0:T(8,128)S(1)} %get-tuple-element.6.refined_ref, f32[16,16]{1,0:T(8,128)S(1)} %get-tuple-element.7.block_ref), custom_call_target="tpu_custom_call" | custom-call | tf_op jit(solution)/shard_map/hand_over/pallas_call | solution.py:402

commit v6 on v4

--- a/solution.py
+++ b/solution.py
@@ -14,6 +14,8 @@
 NEAR_Z = (1, 7, 2, 6)
 RELAYED = ((1, 2, 3), (7, 6, 5), (2, 2, 4))
 ARRIVALS = (1, 7, 2, 6, 3, 5, 4)
+ORDER = [(dy, dz) for dy in (0, 1) for dz in (0,) + ARRIVALS]
+GROUP = 4
 PEERS = sorted(
     [(dy, dz) for dy in (0, 1) for dz in range(Z) if (dy, dz) != (0, 0)],
     key=lambda r: -(2 * r[0] + min(r[1], Z - r[1])),
@@ -112,9 +114,15 @@
     for dz in NEAR_Z:
         send_along(amp_ref, dz, dz)
     loads = []
-    for j in range(tiles):
-        loads.append(pltpu.make_async_copy(fac_hbm.at[:, j], fac.at[j, pl.ds(0, aux)], fac_sem))
-        loads[-1].start()
+    for n, rel in enumerate(ORDER):
+        for m in range(per):
+            j = inner_at(rel, -1) * per + m
+            loads.append(
+                pltpu.make_async_copy(
+                    fac_hbm.at[:, j], fac.at[j, pl.ds(0, aux)], fac_sem.at[n // GROUP]
+                )
+            )
+            loads[-1].start()
     for copy in inputs[1:]:
         copy.wait()
 
@@ -177,20 +185,25 @@
     def piece(who):
         return jnp.concatenate([flat[who * per + m] for m in range(per)], axis=1)
 
-    for c in loads:
-        c.wait()
-
-    def fit(amps, who):
+    def loaded(group):
+        for c in loads[group * GROUP * per : (group + 1) * GROUP * per]:
+            c.wait()
+
+    def fit(amps, rel):
+        n, who = ORDER.index(rel), inner_at(rel, -1)
+        if n % GROUP == 0:
+            loaded(n // GROUP)
         theirs = (amps.astype(jnp.float32) * active_of(who)).astype(jnp.bfloat16)
         return dot(theirs, piece(who), NT)
 
     def fit_along(at):
-        return fit(amp_z[ARRIVALS.index(at)], inner_at((0, at), -1))
+        return fit(amp_z[ARRIVALS.index(at)], (0, at))
 
     def fit_across(at):
         across[at].wait_recv()
-        return fit(amp_yz[ARRIVALS.index(at) + 1 if at else 0], inner_at((1, at), -1))
-
+        return fit(amp_yz[ARRIVALS.index(at) + 1 if at else 0], (1, at))
+
+    loaded(0)
     fitted = dot(masked.astype(jnp.bfloat16), piece(me), NT) + fit_along(1) + fit_along(7)
     for at in (3, 5, 4):
         along[at].wait_recv()
@@ -387,7 +400,7 @@
             pltpu.VMEM((128, 2048), bf),
             pltpu.VMEM((128, 2048), bf),
             sem((8,)),
-            sem,
+            sem((4,)),
             sem((2, N_Z)),
             sem((2, Z)),
             sem((2, Z)),

time: 45.2 us -> 45.2 us (level)
  no operation moved by 1% of the time
where the time goes in v6:
time: 45.2 us; the launch traced here: 45.1 us
  Pallas kernels  44.5 us (98%)
  between operations  0.64 us (1%)
    pallas_call x1, Pallas kernels, local(): pl.pallas_call(kernel, name='exciton', out_shape=(pltpu.VMEM((rows, pairs...  43.8 us

profile of v6, /device:TPU:1, one launch (start us, length us, event | category | flops | bytes accessed | tf_op | source)
XLA Modules:
  0.0 45.1 jit_solution(9423696750721042459)
XLA Ops:
  0.6 43.8 %exciton.1 = (f32[16,768]{1,0:T(8,128)S(1)}, f32[16,16]{1,0:T(8,128)S(1)}) custom-call(bf16[16,768]{1,0:T(8,128)(2,1)} %bitcast.14, bf16[125,96,2,128]{3,2,1,0:T(2,128)(2,1)} %bitcast.12, bf16[128,768]{1,0:T(8,128)(2,1)} %bitcast.13, f32[2,48]{1,0:T(2,128)} %occ_e_hbm.1, f32[2,256]{1,0:T(2,128)} %vir_e_hbm.1, s32[2]{0:T(128)} %occ_n_hbm.1, s32[2]{0:T(128)} %vir_n_hbm.1, ...), custom_call_target="tpu_custom_call" | custom-call | tf_op jit(solution)/shard_map/exciton/pallas_call | solution.py:364
  44.5 0.6 %hand_over.1 = (f32[16,768]{1,0:T(8,128)}, f32[16,1,16]{2,1,0:T(1,128)}) custom-call(f32[16,768]{1,0:T(8,128)S(1)} %get-tuple-element.6.refined_ref, f32[16,16]{1,0:T(8,128)S(1)} %get-tuple-element.7.block_ref), custom_call_target="tpu_custom_call" | custom-call | tf_op jit(solution)/shard_map/hand_over/pallas_call | solution.py:421

commit v7 on v6

--- a/solution.py
+++ b/solution.py
@@ -39,8 +39,9 @@
 
 def inner_at(rel, sign):
     me = lax.axis_index("inner")
+    turn = sign * (1 - 2 * lax.rem(lax.axis_index("grp"), 2))
     y, z = me // Z, me % Z
-    return lax.rem(y + rel[0], 2) * Z + lax.rem(z + sign * rel[1] + Z, Z)
+    return lax.rem(y + rel[0], 2) * Z + lax.rem(z + turn * rel[1] + Z, Z)
 
 
 def grp_at(step, sign):

time: 45.2 us -> 45 us (level)
  no operation moved by 1% of the time
where the time goes in v7:
time: 45 us; the launch traced here: 44.9 us
  Pallas kernels  44.3 us (98%)
  between operations  0.64 us (1%)
    pallas_call x1, Pallas kernels, local(): pl.pallas_call(kernel, name='exciton', out_shape=(pltpu.VMEM((rows, pairs...  43.6 us

profile of v7, /device:TPU:1, one launch (start us, length us, event | category | flops | bytes accessed | tf_op | source)
XLA Modules:
  0.0 44.9 jit_solution(7600012650131202914)
XLA Ops:
  0.6 43.6 %exciton.1 = (f32[16,768]{1,0:T(8,128)S(1)}, f32[16,16]{1,0:T(8,128)S(1)}) custom-call(bf16[16,768]{1,0:T(8,128)(2,1)} %bitcast.14, bf16[125,96,2,128]{3,2,1,0:T(2,128)(2,1)} %bitcast.12, bf16[128,768]{1,0:T(8,128)(2,1)} %bitcast.13, f32[2,48]{1,0:T(2,128)} %occ_e_hbm.1, f32[2,256]{1,0:T(2,128)} %vir_e_hbm.1, s32[2]{0:T(128)} %occ_n_hbm.1, s32[2]{0:T(128)} %vir_n_hbm.1, ...), custom_call_target="tpu_custom_call" | custom-call | tf_op jit(solution)/shard_map/exciton/pallas_call | solution.py:365
  44.3 0.6 %hand_over.1 = (f32[16,768]{1,0:T(8,128)}, f32[16,1,16]{2,1,0:T(1,128)}) custom-call(f32[16,768]{1,0:T(8,128)S(1)} %get-tuple-element.6.refined_ref, f32[16,16]{1,0:T(8,128)S(1)} %get-tuple-element.7.block_ref), custom_call_target="tpu_custom_call" | custom-call | tf_op jit(solution)/shard_map/hand_over/pallas_call | solution.py:422
